TPU v7x, 32 devices: a whole 2x2x4 slice. The times are simulated.
32 devices in a mesh: groups: 2 (over y), wide: 4 (over z), planes: 2 (over x), rep: 2 (over core).
Axes of the slice: x: 2, y: 2, z: 4, core: 2. Of those that a mesh axis runs over, the one named last changes fastest.
Arguments:
- movie_frames: bfloat16 [4, 128, 256, 128], P('planes', ('groups', 'wide'), 'rep'), parts along dimension 1, may hold values from -6 to 6
- pixel_mask: int32 [256, 128], P('rep'), may hold values 0 or 1
- tile_owner: int32 [256, 1], P('rep'), may hold values from 0 to 3; in each aligned block of 128 rows (0 to 127, 128 to 255, ...) at most 48 rows name the same one
- support: int32 [256, 128], P('rep'), may hold values from 0 to 511
- templates: bfloat16 [512, 4, 128], P(None, 'planes'), may hold values from -0.25 to 0.25
- row_taps: float32 [25], replicated, may hold values from -1.25 to 1.25
- col_taps: float32 [25], replicated, may hold values from -1.25 to 1.25
- lag_gains: float32 [4, 3, 65], P('wide'), may hold values from -0.4375 to 0.4375
- dilations: int32 [4, 3], P('wide'), may hold values from 1 to 8
Outputs:
- traces: bfloat16 [128, 128, 256], P('planes', ('groups', 'wide'), 'rep'), parts along dimension 1
- back_projected: bfloat16 [4, 128, 256, 128], P('planes', ('groups', 'wide'), 'rep'), parts along dimension 1
There are 2 independent parts, one for each index of `groups`. A program takes and returns all parts, laid end to end along the dimension named above; an argument that names none is the same for every part. Nothing has to cross between parts.
Inputs may be any that keep to these rules, and one draw needn't show every extreme that they name: Strip h belongs to region class tile_owner[h,0]; the 128 rows of one device name each class at most 48 times.
All inputs are finite; a program needn't handle non-finite values. No bound on the sum of `pixel_mask` on one device may be relied on, other than what follows from the above.
Results may differ from a plain program's by a relative error of at most 0.015.
Values may be sent and summed in bfloat16 or wider, within the bound.
A program may use at most 64 MiB of HBM per device.

v0:
```python
import jax
import jax.numpy as jnp
from jax import lax
from jax.sharding import PartitionSpec as P


def extended(cells, sides, width):
    for axis, dim in sides:
        count = lax.axis_size(axis)
        ends = count - 1
        head = lax.slice_in_dim(cells, 0, width, axis=dim)
        tail = lax.slice_in_dim(cells, cells.shape[dim] - width, cells.shape[dim], axis=dim)
        cells = jnp.concatenate(
            [
                lax.ppermute(tail, axis, [(i, (i + 1) % count) for i in range(ends)]),
                cells,
                lax.ppermute(head, axis, [((i + 1) % count, i) for i in range(ends)]),
            ],
            axis=dim,
        )
    return cells


def band_matrix(tap_values, rows_in, rows_out, sign, offset):
    inner_idx = jnp.arange(rows_in, dtype=jnp.int32)[:, None]
    outer_idx = jnp.arange(rows_out, dtype=jnp.int32)[None, :]
    where_tap = sign * (inner_idx - outer_idx) + offset
    tap_index = jnp.arange(tap_values.shape[0], dtype=jnp.int32)
    picked_taps = where_tap[:, :, None] == tap_index[None, None, :]
    weights = jnp.where(picked_taps, tap_values[None, None, :], jnp.zeros((), tap_values.dtype))
    return jnp.sum(weights, axis=2).astype(jnp.bfloat16)


def lag_matrix(cluster_gains, cluster_lags, frame_count):
    tap_count = cluster_gains.shape[1]
    half_taps = (tap_count - 1) // 2
    lag_values = jnp.arange(2 * frame_count - 1, dtype=jnp.int32) - (frame_count - 1)
    tap_offsets = jnp.arange(tap_count, dtype=jnp.int32) - half_taps
    lag_hits = lag_values[None, :, None] == cluster_lags[:, None, None] * tap_offsets[None, None, :]
    spread = jnp.where(lag_hits, cluster_gains[:, None, :], jnp.zeros((), cluster_gains.dtype))
    kernel = jnp.sum(spread, axis=(0, 2))
    flipped = jnp.concatenate([kernel[::-1], jnp.zeros((1,), kernel.dtype)])
    tiled = jnp.broadcast_to(flipped, (frame_count, 2 * frame_count)).reshape(-1)
    tiled = tiled[: frame_count * (2 * frame_count - 1)].reshape(frame_count, 2 * frame_count - 1)
    return tiled[:, frame_count - 1 :].astype(jnp.bfloat16)


def slot_table(owners, cluster_count, capacity):
    row_count = owners.shape[0]
    owner_marks = (owners[:, None] == jnp.arange(cluster_count, dtype=jnp.int32)[None, :]).astype(
        jnp.int32
    )
    before = jnp.cumsum(owner_marks, axis=0) - owner_marks
    slot_ranks = jnp.sum(before * owner_marks, axis=1)
    slot_of = owners * capacity + slot_ranks
    places = jnp.arange(cluster_count * capacity, dtype=jnp.int32)
    chosen = (slot_of[None, :] == places[:, None]).astype(jnp.int32)
    sources = jnp.sum(chosen * jnp.arange(row_count, dtype=jnp.int32)[None, :], axis=1)
    return (slot_of, sources)


def on_device(
    movie_frames,
    pixel_mask,
    tile_owner,
    support,
    templates,
    row_taps,
    col_taps,
    lag_gains,
    dilations,
):
    planes_here, frames_here, rows_here, col_count = movie_frames.shape
    wide_count = lax.axis_size("wide")
    capacity = max(2, 3 * rows_here // (2 * wide_count))
    rim_width = (row_taps.shape[0] - 1) // 2
    mask_value = pixel_mask.astype(jnp.float32)
    col_fwd = band_matrix(col_taps, col_count, col_count, 1, rim_width)
    smooth = jnp.dot(movie_frames, col_fwd, preferred_element_type=jnp.float32).astype(jnp.bfloat16)
    padded = extended(smooth, (("rep", 2),), rim_width)
    row_fwd = band_matrix(row_taps, rows_here + 2 * rim_width, rows_here, 1, 0)
    along = jnp.einsum("pfew,eh->pfhw", padded, row_fwd, preferred_element_type=jnp.float32)
    filtered = (along * mask_value[None, None]).astype(jnp.bfloat16)
    owners = tile_owner[:, 0]
    slot_of, sources = slot_table(owners, wide_count, capacity)
    packed = jnp.take(filtered, sources, axis=2)
    wide_here = lax.axis_index("wide")
    my_sources = lax.dynamic_slice_in_dim(sources, wide_here * capacity, capacity, 0)
    lag_table = lag_matrix(lag_gains[0], dilations[0], frames_here * wide_count)
    columns = lax.all_to_all(packed, "wide", split_axis=2, concat_axis=1, tiled=True)
    mixed_part = jnp.einsum("pscw,st->ptcw", columns, lag_table, preferred_element_type=jnp.float32)
    columns, mixed_cols = (columns, mixed_part.astype(jnp.bfloat16))
    shapes = jnp.take(templates, jnp.take(support, my_sources, axis=0), axis=0)
    partial_scores = jnp.einsum(
        "cjpw,ptcw->cjt", shapes, mixed_cols, preferred_element_type=jnp.float32
    )
    plane_count = lax.axis_size("planes")
    share_rows = shapes.shape[1] // plane_count
    plane_here = lax.axis_index("planes")
    scores = lax.psum(partial_scores.astype(jnp.bfloat16), "planes").astype(jnp.float32)
    traces = jnp.maximum(scores, 0.0).astype(jnp.bfloat16)
    trace_share = lax.dynamic_slice_in_dim(traces, plane_here * share_rows, share_rows, 1)
    model_part = jnp.einsum("cjpw,cjt->ptcw", shapes, traces, preferred_element_type=jnp.float32)
    slot_masks = jnp.take(mask_value, my_sources, axis=0)
    resid_cols = (columns.astype(jnp.float32) - slot_masks[None, None] * model_part).astype(
        jnp.bfloat16
    )
    resid_back = lax.all_to_all(resid_cols, "wide", split_axis=1, concat_axis=2, tiled=True)
    residual = jnp.take(resid_back, slot_of, axis=2)
    share_back = lax.all_to_all(trace_share, "wide", split_axis=2, concat_axis=0, tiled=True)
    tile_share = jnp.take(share_back, slot_of, axis=0)
    padded_back = extended(residual, (("rep", 2),), rim_width)
    row_adj = band_matrix(row_taps, rows_here + 2 * rim_width, rows_here, -1, 2 * rim_width)
    back_rows = jnp.einsum(
        "pfew,eh->pfhw", padded_back, row_adj, preferred_element_type=jnp.float32
    ).astype(jnp.bfloat16)
    col_adj = band_matrix(col_taps, col_count, col_count, -1, rim_width)
    back_projected = jnp.dot(back_rows, col_adj, preferred_element_type=jnp.float32).astype(
        jnp.bfloat16
    )
    trace_out = jnp.transpose(tile_share, (1, 2, 0))
    return (trace_out, back_projected)


def solution(mesh):
    return jax.shard_map(
        on_device,
        mesh=mesh,
        in_specs=(
            P("planes", ("groups", "wide"), "rep", None),
            P("rep", None),
            P("rep", None),
            P("rep", None),
            P(None, "planes", None),
            P(),
            P(),
            P("wide", None, None),
            P("wide", None),
        ),
        out_specs=(
            P("planes", ("groups", "wide"), "rep"),
            P("planes", ("groups", "wide"), "rep", None),
        ),
        check_vma=False,
    )
```

profile of v0, /device:TPU:0, one launch (start us, length us, event | category | flops | bytes accessed | tf_op | source)
XLA Modules:
  0.0 192.6 jit_solution(7658494077274293809)
XLA Ops:
  7.2 1.1 select_reduce_fusion.2
  8.9 2.4 %collective-permute-start = (bf16[2,16,12,128]{3,2,1,0:T(8,128)(2,1)S(1)}, bf16[2,16,12,128]{3,2,1,0:T(8,128)(2,1)S(1)}, u32[]{:S(2)}, u32[]{:S(2)}) collective-permute-start(bf16[2,16,12,128]{3,2,1,0:T(8,128)(2,1)S(1)} %get-tuple-element.20), channel_id=1, source_target_pairs={{0,1},{2,3},{4,5},{6,7},{8,9},{10,11},{12,13},{14,15},{16,17},{18,... | collective-permute-start | bytes 294920 | tf_op jit(solution)/shard_map/ppermute | solution.py:15
  11.3 1.3 collective-permute-start.1
  13.7 0.8 collective-permute-done.1
  14.5 0.7 fusion.8
  15.2 0.7 copy.43
  15.9 2.1 %gather_fusion.2 = bf16[192,2,16,128]{3,2,1,0:T(8,128)(2,1)} fusion(bf16[2,16,128,128]{3,1,2,0:T(8,128)(2,1)S(1)} %copy.43, s32[1024]{0:T(1024)S(1)} %pad_clamp_fusion.1), kind=kCustom, calls=%fused_computation.2 | custom fusion | bytes 3146496 | tf_op jit(solution)/shard_map/jit(_take)/gather | solution.py:86
  18.0 2.8 %select_bitcast_fusion = bf16[2,16,192,128]{3,1,0,2:T(8,128)(2,1)} fusion(bf16[192,2,16,128]{3,2,1,0:T(8,128)(2,1)} %gather_fusion.2, pred[192]{0:T(512)(128)(4,1)S(1)} %compare_and_fusion.1), kind=kLoop, calls=%fused_computation.23 | loop fusion | flops 786432 | bytes 3145920 | tf_op jit(solution)/shard_map/jit(_take)/select_n | solution.py:86
  20.8 5.8 %all-to-all-start = ((bf16[2,16,192,128]{3,1,0,2:T(8,128)(2,1)}), bf16[2,16,192,128]{3,1,0,2:T(8,128)(2,1)S(1)}, u32[]{:S(2)}, u32[]{:S(2)}) async-start(bf16[2,16,192,128]{3,1,0,2:T(8,128)(2,1)} %select_bitcast_fusion), calls=%async_computation | async-start | bytes 3145728 | tf_op jit(solution)/shard_map/all_to_all | solution.py:90
  27.3 0.6 gather_fusion
  28.0 40.0 %gather_fusion.1 = bf16[6144,2,128]{2,1,0:T(2,128)(2,1)} fusion(bf16[512,2,128]{2,1,0:T(2,128)(2,1)S(1)} %copy-done.1, s32[6144]{0:T(1024)S(1)} %fusion.41), kind=kCustom, calls=%fused_computation.1 | custom fusion | bytes 6316032 | tf_op jit(solution)/shard_map/jit(_take)/gather | solution.py:93
  68.2 1.6 copy.44
  69.8 5.0 %bitcast_convert_fusion = bf16[48,128,64]{1,2,0:T(8,128)(2,1)} fusion(bf16[2,64,48,128]{3,1,0,2:T(8,128)(2,1)} %bitcast.111, bf16[48,128,2,128]{3,2,1,0:T(2,128)(2,1)} %bitcast.107, pred[48,128]{1,0:T(8,128)(4,1)S(1)} %compare_and_fusion, bf16[64,127]{1,0:T(8,128)(2,1)S(1)} %reshape.203), kind=kOutput, calls=%fused_computation.21 | convolution fusion | flops 304742400 | bytes 5527424 | tf_op jit(solution)/shard_map/cjpw,ptcw->cjt/dot_general | solution.py:94
  74.8 0.6 gather_fusion.4
  75.4 35.5 %all-reduce.2.cloned.1.call-done = bf16[48,128,64]{1,2,0:T(8,128)(2,1)} async-done(((bf16[48,128,64]{1,2,0:T(8,128)(2,1)}), bf16[48,128,64]{1,2,0:T(8,128)(2,1)}) %all-reduce.2.cloned.1.call-update) | async-done | bytes 786448 | tf_op jit(solution)/shard_map/psum | solution.py:100
  110.9 1.3 maximum_convert_fusion
  113.0 1.3 reshape.262
  114.4 4.6 %all-to-all-start.1 = ((bf16[4,2,24576]{2,1,0:T(2,128)(2,1)}), bf16[4,2,24576]{2,1,0:T(2,128)(2,1)S(1)}, u32[]{:S(2)}, u32[]{:S(2)}) async-start(bf16[4,2,24576]{2,1,0:T(2,128)(2,1)} %reshape.262), calls=%async_computation.1 | async-start | bytes 786432 | tf_op jit(solution)/shard_map/all_to_all | solution.py:110
  119.0 3.5 %fusion = bf16[2,64,48,128]{3,1,0,2:T(8,128)(2,1)S(1)} fusion(bf16[2,64,48,128]{3,1,0,2:T(8,128)(2,1)S(1)} %bitcast.112, f32[48,128]{1,0:T(8,128)S(1)} %broadcast_select_fusion, bf16[48,128,2,128]{3,2,1,0:T(2,128)(2,1)} %bitcast.108, pred[48,128]{1,0:T(8,128)(4,1)S(1)} %compare_and_fusion, bf16[48,128,64]{1,2,0:T(8,128)(2,1)} %all-reduce.2.cloned.1.call-done), kind=kOutput, calls=%fused_computation.7 | convolution fusion | flops 207224832 | bytes 7108608 | tf_op jit(solution)/shard_map/cjpw,cjt->ptcw/dot_general | solution.py:103
  122.5 2.8 %copy.47 = bf16[2,64,48,128]{3,0,2,1:T(2,128)(2,1)} copy(bf16[2,64,48,128]{3,1,0,2:T(8,128)(2,1)S(1)} %fusion) | data formatting | bytes 3145728 | tf_op jit(solution)/shard_map/convert_element_type | solution.py:105
  125.3 5.2 %all-to-all-done.1 = bf16[4,2,24576]{2,1,0:T(2,128)(2,1)S(1)} async-done(((bf16[4,2,24576]{2,1,0:T(2,128)(2,1)}), bf16[4,2,24576]{2,1,0:T(2,128)(2,1)S(1)}, u32[]{:S(2)}, u32[]{:S(2)}) %all-to-all-start.1) | async-done | bytes 393248 | tf_op jit(solution)/shard_map/all_to_all | solution.py:110
  130.5 4.5 %all-to-all-start.2 = ((bf16[2,64,48,128]{3,0,2,1:T(2,128)(2,1)}), bf16[2,64,48,128]{3,0,2,1:T(2,128)(2,1)}, u32[]{:S(2)}, u32[]{:S(2)}) async-start(bf16[2,64,48,128]{3,0,2,1:T(2,128)(2,1)} %copy.47), calls=%async_computation.2 | async-start | bytes 3145728 | tf_op jit(solution)/shard_map/all_to_all | solution.py:108
  135.8 0.7 gather_fusion.3
  136.5 34.9 %all-to-all-done.2 = bf16[2,64,48,128]{3,0,2,1:T(2,128)(2,1)} async-done(((bf16[2,64,48,128]{3,0,2,1:T(2,128)(2,1)}), bf16[2,64,48,128]{3,0,2,1:T(2,128)(2,1)}, u32[]{:S(2)}, u32[]{:S(2)}) %all-to-all-start.2) | async-done | bytes 1572896 | tf_op jit(solution)/shard_map/all_to_all | solution.py:108
  171.4 1.6 copy.48
  173.2 1.0 copy.50
  174.2 1.7 gather_fusion.5
  176.0 1.7 fusion.26
  177.7 1.9 %collective-permute-start.2 = (bf16[2,16,12,128]{3,2,1,0:T(8,128)(2,1)S(1)}, bf16[2,16,12,128]{3,2,1,0:T(8,128)(2,1)}, u32[]{:S(2)}, u32[]{:S(2)}) collective-permute-start(bf16[2,16,12,128]{3,2,1,0:T(8,128)(2,1)S(1)} %get-tuple-element.18), channel_id=1, source_target_pairs={{0,1},{2,3},{4,5},{6,7},{8,9},{10,11},{12,13},{14,15},{16,17},{18,... | collective-permute-start | bytes 294920 | tf_op jit(solution)/shard_map/ppermute | solution.py:15
  179.7 1.3 collective-permute-start.3
  181.2 1.3 copy.52
  183.0 2.8 %convolution_convert_fusion.1 = bf16[2,16,128,128]{3,2,1,0:T(8,128)(2,1)} fusion(bf16[2,16,12,128]{3,2,1,0:T(8,128)(2,1)} %collective-permute-done.3, bf16[2,16,128,128]{3,2,1,0:T(8,128)(2,1)S(1)} %fusion.26, bf16[2,16,12,128]{3,2,1,0:T(8,128)(2,1)} %collective-permute-done.2, bf16[152,128]{1,0:T(8,128)(2,1)S(1)} %get-tuple-element.12, ...), kind=kOutput, calls=%fused_computation.27 | convolution fusion | flops 298385408 | bytes 2365440 | tf_op jit(solution)/shard_map/dot_general | solution.py:118
  (61 shorter events, 5.1 us)
Async XLA Ops:
  7.2 1.2 copy-start
  7.2 5.4 %copy-start.5 = (s32[128,1]{0,1:T(1,128)S(1)}, s32[128,1]{0,1:T(1,128)}, u32[]{:S(2)}) copy-start(s32[128,1]{0,1:T(1,128)} %param.11) | copy-start | bytes 1540
  7.2 6.0 %copy-start.4 = (s32[128,128]{1,0:T(8,128)S(1)}, s32[128,128]{1,0:T(8,128)}, u32[]{:S(2)}) copy-start(s32[128,128]{1,0:T(8,128)} %param.10) | copy-start | bytes 196612
  8.4 4.9 %copy-start.7 = (f32[25]{0:T(128)S(1)}, f32[25]{0:T(128)}, u32[]{:S(2)}) copy-start(f32[25]{0:T(128)} %param.14) | copy-start | bytes 304
  8.9 4.8 %collective-permute-start = (bf16[2,16,12,128]{3,2,1,0:T(8,128)(2,1)S(1)}, bf16[2,16,12,128]{3,2,1,0:T(8,128)(2,1)S(1)}, u32[]{:S(2)}, u32[]{:S(2)}) collective-permute-start(bf16[2,16,12,128]{3,2,1,0:T(8,128)(2,1)S(1)} %get-tuple-element.20), channel_id=1, source_target_pairs={{0,1},{2,3},{4,5},{6,7},{8,9},{10,11},{12,13},{14,15},{16,17},{18,... | collective-permute-start | bytes 294920 | tf_op jit(solution)/shard_map/ppermute | solution.py:15
  11.3 3.2 %collective-permute-start.1 = (bf16[2,16,12,128]{3,2,1,0:T(8,128)(2,1)S(1)}, bf16[2,16,12,128]{3,2,1,0:T(8,128)(2,1)S(1)}, u32[]{:S(2)}, u32[]{:S(2)}) collective-permute-start(bf16[2,16,12,128]{3,2,1,0:T(8,128)(2,1)S(1)} %get-tuple-element.21), channel_id=1, source_target_pairs={{1,0},{3,2},{5,4},{7,6},{9,8},{11,10},{13,12},{15,14},{17,16},{19,... | collective-permute-start | bytes 294920 | tf_op jit(solution)/shard_map/ppermute | solution.py:17
  20.8 5.9 %copy-start.6 = (f32[1,3,65]{2,0,1:T(1,128)S(1)}, f32[1,3,65]{2,0,1:T(1,128)}, u32[]{:S(2)}) copy-start(f32[1,3,65]{2,0,1:T(1,128)} %param.16) | copy-start | bytes 2344
  20.8 5.9 %copy-start.8 = (s32[1,3]{1,0:T(1,128)S(1)}, s32[1,3]{1,0:T(1,128)}, u32[]{:S(2)}) copy-start(s32[1,3]{1,0:T(1,128)} %param.17) | copy-start | bytes 40
  20.8 6.5 %copy-start.3 = (s32[128,128]{1,0:T(8,128)S(1)}, s32[128,128]{1,0:T(8,128)}, u32[]{:S(2)}) copy-start(s32[128,128]{1,0:T(8,128)} %param.12) | copy-start | bytes 196612
  20.8 7.2 %copy-start.1 = (bf16[512,2,128]{2,1,0:T(2,128)(2,1)S(1)}, bf16[512,2,128]{2,1,0:T(2,128)(2,1)}, u32[]{:S(2)}) copy-start(bf16[512,2,128]{2,1,0:T(2,128)(2,1)} %param.13) | copy-start | bytes 786436
  20.8 47.4 %all-to-all-start = ((bf16[2,16,192,128]{3,1,0,2:T(8,128)(2,1)}), bf16[2,16,192,128]{3,1,0,2:T(8,128)(2,1)S(1)}, u32[]{:S(2)}, u32[]{:S(2)}) async-start(bf16[2,16,192,128]{3,1,0,2:T(8,128)(2,1)} %select_bitcast_fusion), calls=%async_computation | async-start | bytes 3145728 | tf_op jit(solution)/shard_map/all_to_all | solution.py:90
  26.6 84.2 %all-reduce.2.cloned.1.call-start = ((), (), s32[]{:S(2)}) async-start(), calls=%async_computation.3 | async-start | bytes 1572864 | tf_op jit(solution)/shard_map/psum | solution.py:100
  112.5 6.5 %copy-start.2 = (bf16[2,16,4,48,128]{4,1,2,0,3:T(8,128)(2,1)S(1)}, bf16[2,16,4,48,128]{4,1,2,0,3:T(8,128)(2,1)}, u32[]{:S(2)}) copy-start(bf16[2,16,4,48,128]{4,1,2,0,3:T(8,128)(2,1)} %copy.44) | copy-start | bytes 4718596
  114.4 16.1 %all-to-all-start.1 = ((bf16[4,2,24576]{2,1,0:T(2,128)(2,1)}), bf16[4,2,24576]{2,1,0:T(2,128)(2,1)S(1)}, u32[]{:S(2)}, u32[]{:S(2)}) async-start(bf16[4,2,24576]{2,1,0:T(2,128)(2,1)} %reshape.262), calls=%async_computation.1 | async-start | bytes 786432 | tf_op jit(solution)/shard_map/all_to_all | solution.py:110
  130.5 40.9 %all-to-all-start.2 = ((bf16[2,64,48,128]{3,0,2,1:T(2,128)(2,1)}), bf16[2,64,48,128]{3,0,2,1:T(2,128)(2,1)}, u32[]{:S(2)}, u32[]{:S(2)}) async-start(bf16[2,64,48,128]{3,0,2,1:T(2,128)(2,1)} %copy.47), calls=%async_computation.2 | async-start | bytes 3145728 | tf_op jit(solution)/shard_map/all_to_all | solution.py:108
  177.7 4.7 %collective-permute-start.2 = (bf16[2,16,12,128]{3,2,1,0:T(8,128)(2,1)S(1)}, bf16[2,16,12,128]{3,2,1,0:T(8,128)(2,1)}, u32[]{:S(2)}, u32[]{:S(2)}) collective-permute-start(bf16[2,16,12,128]{3,2,1,0:T(8,128)(2,1)S(1)} %get-tuple-element.18), channel_id=1, source_target_pairs={{0,1},{2,3},{4,5},{6,7},{8,9},{10,11},{12,13},{14,15},{16,17},{18,... | collective-permute-start | bytes 294920 | tf_op jit(solution)/shard_map/ppermute | solution.py:15
  179.7 3.4 %collective-permute-start.3 = (bf16[2,16,12,128]{3,2,1,0:T(8,128)(2,1)S(1)}, bf16[2,16,12,128]{3,2,1,0:T(8,128)(2,1)}, u32[]{:S(2)}, u32[]{:S(2)}) collective-permute-start(bf16[2,16,12,128]{3,2,1,0:T(8,128)(2,1)S(1)} %get-tuple-element.19), channel_id=1, source_target_pairs={{1,0},{3,2},{5,4},{7,6},{9,8},{11,10},{13,12},{15,14},{17,16},{19,... | collective-permute-start | bytes 294920 | tf_op jit(solution)/shard_map/ppermute | solution.py:17
Sparse Core Ops, SparseCore 0:
  74.9 35.8 all-reduce.1
where the time goes:
time: 194 us; the launch traced here: 193 us
  waiting for transfers between devices  77 us (40%)
  local copies, waits for them, and re-layouts  58.1 us (30%)
  starting transfers between devices  21.9 us (11%)
  between operations  14.4 us (7%)
  matrix products  12.3 us (6%)
  other arithmetic  8.88 us (5%)
    gather x2, local copies, waits for them, and re-layouts, on_device(): shapes = jnp.take(templates, jnp.take(support, my_sources, axis=0), axis=0)  40.6 us
    psum x1, waiting for transfers between devices, on_device(): lax.psum(partial_scores.astype(jnp.bfloat16), 'planes').astype(jnp.float32)  35.5 us
    all_to_all x1, waiting for transfers between devices, on_device(): lax.all_to_all(resid_cols, 'wide', split_axis=1, concat_axis=2, tiled=True)  34.9 us
    all_to_all x1, starting transfers between devices, on_device(): lax.all_to_all(packed, 'wide', split_axis=2, concat_axis=1, tiled=True)  5.83 us
    all_to_all x1, waiting for transfers between devices, on_device(): lax.all_to_all(trace_share, 'wide', split_axis=2, concat_axis=0, tiled=True)  5.2 us
    dot_general x1, matrix products, on_device(): jnp.einsum('cjpw,ptcw->cjt', shapes, mixed_cols, preferred_element_type=j...  5.01 us
    all_to_all x1, starting transfers between devices, on_device(): lax.all_to_all(trace_share, 'wide', split_axis=2, concat_axis=0, tiled=True)  4.6 us
    all_to_all x1, starting transfers between devices, on_device(): lax.all_to_all(resid_cols, 'wide', split_axis=1, concat_axis=2, tiled=True)  4.53 us
  transfers between devices with their start and end apart: 8, of which 5 were waited for; matrix products, arithmetic and copies ran while one was open for 27% of the time, Pallas kernels for 0%

commit v1 on v0

v1 whole, which is shorter than its diff:
```python
import functools

import jax
import jax.numpy as jnp
from jax import lax
from jax.experimental import pallas as pl
from jax.experimental.pallas import tpu as pltpu
from jax.sharding import PartitionSpec as P

MESH = pl.DeviceIdType.MESH
BF = jnp.bfloat16
F32 = jnp.float32


def extended(cells, axis, dim, width):
    count = lax.axis_size(axis)
    ends = count - 1
    head = lax.slice_in_dim(cells, 0, width, axis=dim)
    tail = lax.slice_in_dim(cells, cells.shape[dim] - width, cells.shape[dim], axis=dim)
    return jnp.concatenate(
        [
            lax.ppermute(tail, axis, [(i, (i + 1) % count) for i in range(ends)]),
            cells,
            lax.ppermute(head, axis, [((i + 1) % count, i) for i in range(ends)]),
        ],
        axis=dim,
    )


def band_matrix(tap_values, rows_in, rows_out, sign, offset):
    inner_idx = jnp.arange(rows_in, dtype=jnp.int32)[:, None]
    outer_idx = jnp.arange(rows_out, dtype=jnp.int32)[None, :]
    where_tap = sign * (inner_idx - outer_idx) + offset
    tap_index = jnp.arange(tap_values.shape[0], dtype=jnp.int32)
    picked_taps = where_tap[:, :, None] == tap_index[None, None, :]
    weights = jnp.where(picked_taps, tap_values[None, None, :], jnp.zeros((), tap_values.dtype))
    return jnp.sum(weights, axis=2).astype(BF)


def lag_matrix(cluster_gains, cluster_lags, frame_count):
    tap_count = cluster_gains.shape[1]
    half_taps = (tap_count - 1) // 2
    lag_values = jnp.arange(2 * frame_count - 1, dtype=jnp.int32) - (frame_count - 1)
    tap_offsets = jnp.arange(tap_count, dtype=jnp.int32) - half_taps
    lag_hits = lag_values[None, :, None] == cluster_lags[:, None, None] * tap_offsets[None, None, :]
    spread = jnp.where(lag_hits, cluster_gains[:, None, :], jnp.zeros((), cluster_gains.dtype))
    kernel = jnp.sum(spread, axis=(0, 2))
    padded = jnp.concatenate([kernel, jnp.zeros((1,), kernel.dtype)])
    tiled = jnp.broadcast_to(padded, (frame_count, 2 * frame_count)).reshape(-1)
    tiled = tiled[: frame_count * (2 * frame_count - 1)].reshape(frame_count, 2 * frame_count - 1)
    return tiled[:, frame_count - 1 :].astype(BF)


def mid_kernel(
    f_ref, sup_ref, own_ref, temp_ref, lag_ref, mask_ref,
    res_ref, tr_ref,
    hot, pall, part, xrecv, zsend, gath, lag_all, tbuf, tr_all, fold,
    lag_s, lag_r, x1_s, x1_r, z1_s, z1_r, z2_s, z2_r, x2_s, x2_r,
):
    np_ = lax.axis_size("planes")
    nw = lax.axis_size("wide")
    p = lax.axis_index("planes")
    z = lax.axis_index("wide")
    blocks, hb, frames, comps = part.shape
    shapes = temp_ref.shape[0]
    tile = min(256, shapes)
    total = nw * frames

    barrier = pltpu.get_barrier_semaphore()
    for k in range(1, nw):
        pl.semaphore_signal(barrier, inc=1, device_id={"wide": lax.rem(z + k, nw)}, device_id_type=MESH)
    for k in range(1, np_):
        pl.semaphore_signal(barrier, inc=1, device_id={"planes": lax.rem(p + k, np_)}, device_id_type=MESH)
    pl.semaphore_wait(barrier, nw - 1 + np_ - 1)

    def to_wide(src, dst, send, recv, k):
        return pltpu.make_async_remote_copy(
            src_ref=src, dst_ref=dst, send_sem=send.at[k - 1], recv_sem=recv.at[k - 1],
            device_id={"wide": lax.rem(z + k, nw)}, device_id_type=MESH)

    def to_plane(src, dst, send, recv, dp, zi):
        slot = (dp - 1) * nw + zi
        return pltpu.make_async_remote_copy(
            src_ref=src, dst_ref=dst, send_sem=send.at[slot], recv_sem=recv.at[slot],
            device_id={"planes": lax.rem(p + dp, np_)}, device_id_type=MESH)

    def lag_copy(k):
        return to_wide(lag_ref, lag_all.at[z], lag_s, lag_r, k)

    def x1_copy(dp, zi):
        return to_plane(part.at[lax.rem(p + dp, np_) * nw + zi], xrecv.at[(dp - 1) * nw + zi], x1_s, x1_r, dp, zi)

    def z1_copy(k):
        return to_wide(zsend.at[lax.rem(z + k, nw)], gath.at[z], z1_s, z1_r, k)

    def z2_copy(k):
        return to_wide(tbuf.at[lax.rem(z + k, nw)], tr_all.at[p * nw + z], z2_s, z2_r, k)

    def x2_copy(dp, zi):
        return to_plane(tr_all.at[p * nw + zi], tr_all.at[p * nw + zi], x2_s, x2_r, dp, zi)

    for k in range(1, nw):
        lag_copy(k).start()
    lag_all[z] = lag_ref[...]

    ids = lax.broadcasted_iota(jnp.int32, (tile, comps), 0)

    def project(b):
        base = b * hb
        f_blk = f_ref[pl.ds(base, hb)].reshape(hb * frames, f_ref.shape[2])
        pall[...] = lax.dot_general(
            f_blk, temp_ref[...], (((1,), (1,)), ((), ())), preferred_element_type=F32).astype(BF)
        sup = sup_ref[b]
        for i in range(hb):
            row = sup[i : i + 1, :]
            for q in range(0, shapes, tile):
                hot[base + i, q : q + tile, :] = jnp.where(ids == row - q, 1.0, 0.0).astype(BF)
            part[b, i] = jnp.dot(
                pall[i * frames : (i + 1) * frames, :], hot[base + i], preferred_element_type=F32).astype(BF)

    def others(n, carry):
        dp = n // nw + 1
        zi = lax.rem(z + 1 + n, nw)
        project(lax.rem(p + dp, np_) * nw + zi)
        x1_copy(dp, zi).start()
        return carry

    lax.fori_loop(0, (np_ - 1) * nw, others, 0)

    def mine(n, carry):
        zi = lax.rem(z + 1 + n, nw)
        b = p * nw + zi
        project(b)
        acc = part[b].astype(F32)
        for dp in range(1, np_):
            x1_copy(dp, zi).wait_recv()
            acc = acc + xrecv[(dp - 1) * nw + zi].astype(F32)
        zsend[zi] = acc.astype(BF)

        @pl.when(n < nw - 1)
        def _():
            z1_copy(n + 1).start()

        return carry

    lax.fori_loop(0, nw, mine, 0)
    gath[z] = zsend[z]

    def arrived(k, carry):
        lag_copy(k).wait()
        z1_copy(k).wait()
        return carry

    lax.fori_loop(1, nw, arrived, 0)

    me = p * nw + z
    for i in range(hb):
        table = lag_all[own_ref[me * hb + i]]
        columns = gath[:, i].reshape(total, comps)
        scores = jnp.dot(table, columns, preferred_element_type=F32)
        tbuf[:, i] = jnp.maximum(scores, 0.0).astype(BF).reshape(nw, frames, comps)

    def give(k, carry):
        z2_copy(k).start()
        return carry

    lax.fori_loop(1, nw, give, 0)
    tr_all[me] = tbuf[z]

    def model(b):
        base = b * hb
        for i in range(hb):
            fold[i * frames : (i + 1) * frames, :] = lax.dot_general(
                tr_all[b, i], hot[base + i], (((1,), (1,)), ((), ())), preferred_element_type=F32).astype(BF)
        out = jnp.dot(fold[...], temp_ref[...], preferred_element_type=F32)
        out = out.reshape(hb, frames, out.shape[1])
        mask = mask_ref[pl.ds(base, hb)]
        res_ref[pl.ds(base, hb)] = (f_ref[pl.ds(base, hb)].astype(F32) - mask * out).astype(BF)

    def same_plane(k, carry):
        zi = lax.rem(z + nw - k, nw)

        @pl.when(k > 0)
        def _():
            z2_copy(lax.max(k, 1)).wait_recv()

        for dp in range(1, np_):
            x2_copy(dp, zi).start()
        model(p * nw + zi)
        return carry

    lax.fori_loop(0, nw, same_plane, 0)

    def other_planes(n, carry):
        dp = n // nw + 1
        zi = lax.rem(z + nw - lax.rem(n, nw), nw)
        x2_copy(dp, zi).wait_recv()
        model(lax.rem(p + np_ - dp, np_) * nw + zi)
        return carry

    lax.fori_loop(0, (np_ - 1) * nw, other_planes, 0)
    tr_ref[...] = tr_all[...]

    def drained_planes(n, carry):
        x1_copy(n // nw + 1, lax.rem(n, nw)).wait_send()
        x2_copy(n // nw + 1, lax.rem(n, nw)).wait_send()
        return carry

    lax.fori_loop(0, (np_ - 1) * nw, drained_planes, 0)

    def drained_wide(k, carry):
        z2_copy(k).wait_send()
        return carry

    lax.fori_loop(1, nw, drained_wide, 0)


def middle(filtered, support, owners, shapes, lag_table, mask):
    np_ = lax.axis_size("planes")
    nw = lax.axis_size("wide")
    blocks = np_ * nw
    rows, frames, pixels = filtered.shape
    hb = rows // blocks
    comps = support.shape[1]
    count = shapes.shape[0]
    total = nw * frames
    vm = pl.BlockSpec(memory_space=pltpu.VMEM)
    dma = pltpu.SemaphoreType.DMA
    piece = (hb, frames, comps)
    res, tr = pl.pallas_call(
        mid_kernel,
        out_shape=(
            jax.ShapeDtypeStruct(filtered.shape, BF),
            jax.ShapeDtypeStruct((blocks,) + piece, BF),
        ),
        in_specs=[vm, vm, pl.BlockSpec(memory_space=pltpu.SMEM), vm, vm, vm],
        out_specs=(vm, vm),
        scratch_shapes=[
            pltpu.VMEM((rows, count, comps), BF),
            pltpu.VMEM((hb * frames, count), BF),
            pltpu.VMEM((blocks,) + piece, BF),
            pltpu.VMEM(((np_ - 1) * nw,) + piece, BF),
            pltpu.VMEM((nw,) + piece, BF),
            pltpu.VMEM((nw,) + piece, BF),
            pltpu.VMEM((nw, total, total), BF),
            pltpu.VMEM((nw,) + piece, BF),
            pltpu.VMEM((blocks,) + piece, BF),
            pltpu.VMEM((hb * frames, count), BF),
            dma((nw - 1,)), dma((nw - 1,)),
            dma(((np_ - 1) * nw,)), dma(((np_ - 1) * nw,)),
            dma((nw - 1,)), dma((nw - 1,)),
            dma((nw - 1,)), dma((nw - 1,)),
            dma(((np_ - 1) * nw,)), dma(((np_ - 1) * nw,)),
        ],
        compiler_params=pltpu.CompilerParams(
            collective_id=0, has_side_effects=True, vmem_limit_bytes=60 * 1024 * 1024
        ),
    )(filtered, support.reshape(blocks, hb, comps), owners, shapes, lag_table, mask)
    return res, tr.reshape(rows, frames, comps)


def on_device(
    movie_frames, pixel_mask, tile_owner, support, templates, row_taps, col_taps, lag_gains, dilations
):
    planes_here, frames_here, rows_here, col_count = movie_frames.shape
    nw = lax.axis_size("wide")
    rim = (row_taps.shape[0] - 1) // 2
    mask_value = pixel_mask.astype(F32)
    col_fwd = band_matrix(col_taps, col_count, col_count, 1, rim)
    smooth = jnp.dot(movie_frames, col_fwd, preferred_element_type=F32).astype(BF)
    padded = extended(smooth, "rep", 2, rim)
    row_fwd = band_matrix(row_taps, rows_here + 2 * rim, rows_here, 1, 0)
    along = jnp.einsum("pfew,eh->hfpw", padded, row_fwd, preferred_element_type=F32)
    filtered = (along * mask_value[:, None, None, :]).astype(BF)
    filtered = filtered.reshape(rows_here, frames_here, planes_here * col_count)
    lag_table = lag_matrix(lag_gains[0], dilations[0], frames_here * nw)
    wide_mask = jnp.tile(mask_value, (1, planes_here))[:, None, :]
    shapes = templates.reshape(templates.shape[0], planes_here * col_count)
    residual, traces = middle(filtered, support, tile_owner[:, 0], shapes, lag_table, wide_mask)

    padded_back = extended(residual, "rep", 0, rim)
    padded_back = padded_back.reshape(rows_here + 2 * rim, frames_here, planes_here, col_count)
    row_adj = band_matrix(row_taps, rows_here + 2 * rim, rows_here, -1, 2 * rim)
    back_rows = jnp.einsum("efpw,eh->pfhw", padded_back, row_adj, preferred_element_type=F32).astype(BF)
    col_adj = band_matrix(col_taps, col_count, col_count, -1, rim)
    back_projected = jnp.dot(back_rows, col_adj, preferred_element_type=F32).astype(BF)

    share = traces.shape[2] // lax.axis_size("planes")
    mine = lax.dynamic_slice_in_dim(traces, lax.axis_index("planes") * share, share, 2)
    return (jnp.transpose(mine, (2, 1, 0)), back_projected)


def solution(mesh):
    return jax.shard_map(
        on_device,
        mesh=mesh,
        in_specs=(
            P("planes", ("groups", "wide"), "rep", None),
            P("rep", None),
            P("rep", None),
            P("rep", None),
            P(None, "planes", None),
            P(),
            P(),
            P("wide", None, None),
            P("wide", None),
        ),
        out_specs=(
            P("planes", ("groups", "wide"), "rep"),
            P("planes", ("groups", "wide"), "rep", None),
        ),
        check_vma=False,
    )
```

time: 194 us -> 60.7 us (0.31)
  the two profiles are of different devices: /device:TPU:0 before, /device:TPU:1 now
where the time goes in v1:
time: 60.7 us; the launch traced here: 60.3 us
  Pallas kernels  28.6 us (47%)
  starting transfers between devices  11 us (18%)
  local copies, waits for them, and re-layouts  10.1 us (17%)
  matrix products  5.43 us (9%)
  other arithmetic  4.26 us (7%)
  between operations  0.83 us (1%)
    pallas_call x1, Pallas kernels, middle(): pl.pallas_call(mid_kernel, out_shape=(jax.ShapeDtypeStruct(filtered.shape...  28.6 us
    ppermute x2, starting transfers between devices, extended(): lax.ppermute(head, axis, [((i + 1) % count, i) for i in range(ends)])  8.46 us
    unnamed x21, local copies, waits for them, and re-layouts  3.35 us
    dot_general x1, matrix products, on_device(): jnp.dot(back_rows, col_adj, preferred_element_type=F32).astype(BF)  3.07 us
    reduce_sum x2, other arithmetic, band_matrix(): return jnp.sum(weights, axis=2).astype(BF)  2.83 us
    ppermute x2, starting transfers between devices, extended(): lax.ppermute(tail, axis, [(i, (i + 1) % count) for i in range(ends)])  2.58 us
    dot_general x1, matrix products, on_device(): jnp.einsum('pfew,eh->hfpw', padded, row_fwd, preferred_element_type=F32)  1.94 us
    reshape x1, local copies, waits for them, and re-layouts, on_device(): filtered = filtered.reshape(rows_here, frames_here, planes_here * col_count)  1.49 us
  transfers between devices with their start and end apart: 4, of which 0 were waited for; matrix products, arithmetic and copies ran while one was open for 9% of the time, Pallas kernels for 0%

profile of v1, /device:TPU:1, one launch (start us, length us, event | category | flops | bytes accessed | tf_op | source)
XLA Modules:
  0.0 60.3 jit_solution(15446643833254131974)
XLA Ops:
  0.6 0.0 copy-start
  0.7 1.7 %select_reduce_fusion.2 = (bf16[128,128]{1,0:T(8,128)(2,1)}, bf16[128,128]{1,0:T(8,128)(2,1)S(1)}) fusion(s32[128,128]{1,0:T(8,128)S(1)} %get-tuple-element.14, f32[25]{0:T(128)} %param.15, s32[128,128]{1,0:T(8,128)S(1)} %get-tuple-element.15), kind=kLoop, calls=%fused_computation.5 | loop fusion | flops 2424832 | bytes 196708 | tf_op jit(solution)/shard_map/reduce_sum | solution.py:37
  2.4 0.0 copy-start.3
  2.4 0.0 copy-start.2
  2.5 0.4 fusion.1
  2.9 1.3 %collective-permute-start = (bf16[2,16,12,128]{3,2,1,0:T(8,128)(2,1)S(1)}, bf16[2,16,12,128]{3,2,1,0:T(8,128)(2,1)S(1)}, u32[]{:S(2)}, u32[]{:S(2)}) collective-permute-start(bf16[2,16,12,128]{3,2,1,0:T(8,128)(2,1)S(1)} %get-tuple-element.12), channel_id=1, source_target_pairs={{0,1},{2,3},{4,5},{6,7},{8,9},{10,11},{12,13},{14,15},{16,17},{18,... | collective-permute-start | bytes 294920 | tf_op jit(solution)/shard_map/ppermute | solution.py:22
  4.2 3.0 %collective-permute-start.1 = (bf16[2,16,12,128]{3,2,1,0:T(8,128)(2,1)S(1)}, bf16[2,16,12,128]{3,2,1,0:T(8,128)(2,1)S(1)}, u32[]{:S(2)}, u32[]{:S(2)}) collective-permute-start(bf16[2,16,12,128]{3,2,1,0:T(8,128)(2,1)S(1)} %get-tuple-element.13), channel_id=1, source_target_pairs={{1,0},{3,2},{5,4},{7,6},{9,8},{11,10},{13,12},{15,14},{17,16},{19,... | collective-permute-start | bytes 294920 | tf_op jit(solution)/shard_map/ppermute | solution.py:24
  7.4 0.1 broadcast_multiply_fusion
  7.4 0.1 select_reduce_fusion.4
  7.6 0.1 maximum_convert_fusion
  7.7 1.1 %select_reduce_fusion = (bf16[152,128]{1,0:T(8,128)(2,1)}, bf16[152,128]{1,0:T(8,128)(2,1)}) fusion(s32[152,128]{1,0:T(8,128)S(1)} %get-tuple-element.16, f32[25]{0:T(128)S(1)} %copy-done.5, s32[152,128]{1,0:T(8,128)S(1)} %get-tuple-element.17), kind=kLoop, calls=%fused_computation.1 | loop fusion | flops 2879488 | bytes 233572 | tf_op jit(solution)/shard_map/reduce_sum | solution.py:37
  8.7 0.1 copy.14
  8.8 0.7 %copy.29 = bf16[64,8,2,128]{3,1,2,0:T(8,128)(2,1)} copy(bf16[64,8,2,128]{3,2,1,0:T(2,128)(2,1)S(1)} %bitcast.48) | data formatting | bytes 524288
  9.6 0.2 reshape.128
  9.7 0.7 %slice.29.lag_ref = bf16[64,64]{1,0:T(8,128)(2,1)} slice(bf16[64,127]{1,0:T(8,128)(2,1)S(1)} %reshape.128), slice={[0:64], [63:127]} | slice | bytes 16384 | tf_op jit(solution)/shard_map/slice | solution.py:51
  10.4 0.0 collective-permute-done
  10.4 0.0 collective-permute-done.1
  10.4 0.6 %copy-done.7 = bf16[2,16,12,128]{3,2,1,0:T(8,128)(2,1)} copy-done((bf16[2,16,12,128]{3,2,1,0:T(8,128)(2,1)}, bf16[2,16,12,128]{3,2,1,0:T(8,128)(2,1)S(1)}, u32[]{:S(2)}) %copy-start.7) | copy-done | bytes 98328
  11.1 0.7 %copy-done.8 = bf16[2,16,12,128]{3,2,1,0:T(8,128)(2,1)} copy-done((bf16[2,16,12,128]{3,2,1,0:T(8,128)(2,1)}, bf16[2,16,12,128]{3,2,1,0:T(8,128)(2,1)S(1)}, u32[]{:S(2)}) %copy-start.8) | copy-done | bytes 98328
  11.7 1.9 %fusion = bf16[128,16,2,128]{0,3,1,2:T(8,128)(2,1)S(1)} fusion(bf16[2,16,12,128]{3,2,1,0:T(8,128)(2,1)} %copy-done.8, bf16[2,16,128,128]{3,2,1,0:T(8,128)(2,1)S(1)} %fusion.1, bf16[2,16,12,128]{3,2,1,0:T(8,128)(2,1)} %copy-done.7, f32[128,128]{0,1:T(8,128)S(1)} %copy.14, bf16[152,128]{1,0:T(8,128)(2,1)} %get-tuple-element.9), kind=kOutput, calls=%fused_computation.12 | convolution fusion | flops 164167680 | bytes 2398208 | tf_op jit(solution)/shard_map/pfew,eh->hfpw/dot_general | solution.py:273
  13.7 1.0 %copy.15 = bf16[128,16,2,128]{3,2,1,0:T(2,128)(2,1)S(1)} copy(bf16[128,16,2,128]{0,3,1,2:T(8,128)(2,1)S(1)} %fusion) | data formatting | bytes 2097152 | tf_op jit(solution)/shard_map/convert_element_type | solution.py:274
  14.7 1.5 %reshape.124.f_ref = bf16[128,16,256]{2,1,0:T(8,128)(2,1)} reshape(bf16[128,16,2,128]{3,2,1,0:T(2,128)(2,1)S(1)} %copy.15) | data formatting | bytes 2097152 | tf_op jit(solution)/shard_map/reshape | solution.py:275
  16.2 0.7 %tile.8 = f32[128,2,128]{2,1,0:T(2,128)} broadcast(f32[128,128]{1,0:T(8,128)S(1)} %convert_element_type.41), dimensions={0,2} | broadcast | bytes 196608 | tf_op jit(solution)/shard_map/tile | solution.py:277
  16.9 28.6 %shard_map.104 = (bf16[128,16,256]{2,1,0:T(8,128)(2,1)}, bf16[8,16,16,128]{3,2,1,0:T(8,128)(2,1)}) custom-call(bf16[128,16,256]{2,1,0:T(8,128)(2,1)} %reshape.124.f_ref, s32[8,16,128]{2,1,0:T(8,128)} %bitcast.49, s32[128]{0:T(128)} %bitcast.52, bf16[512,256]{1,0:T(8,128)(2,1)} %bitcast.44, bf16[64,64]{1,0:T(8,128)(2,1)} %slice.29.lag_ref, ...), custom_call_target="tpu_custom_call" | custom-call | tf_op jit(solution)/shard_map/pallas_call | solution.py:230
  45.5 1.0 %fusion.22 = (bf16[12,16,256]{2,1,0:T(8,128)(2,1)S(1)}, bf16[12,16,256]{2,1,0:T(8,128)(2,1)S(1)}) fusion(bf16[128,16,256]{2,1,0:T(8,128)(2,1)} %get-tuple-element.5), kind=kLoop, calls=%fused_computation.45 | loop fusion | bytes 393216 | tf_op jit(solution)/shard_map/slice | solution.py:19
  46.5 1.3 %collective-permute-start.2 = (bf16[12,16,256]{2,1,0:T(8,128)(2,1)S(1)}, bf16[12,16,256]{2,1,0:T(8,128)(2,1)}, u32[]{:S(2)}, u32[]{:S(2)}) collective-permute-start(bf16[12,16,256]{2,1,0:T(8,128)(2,1)S(1)} %get-tuple-element.10), channel_id=1, source_target_pairs={{0,1},{2,3},{4,5},{6,7},{8,9},{10,11},{12,13},{14,15},{16,17},{18,... | collective-permute-start | bytes 294920 | tf_op jit(solution)/shard_map/ppermute | solution.py:22
  47.8 5.4 %collective-permute-start.3 = (bf16[12,16,256]{2,1,0:T(8,128)(2,1)S(1)}, bf16[12,16,256]{2,1,0:T(8,128)(2,1)}, u32[]{:S(2)}, u32[]{:S(2)}) collective-permute-start(bf16[12,16,256]{2,1,0:T(8,128)(2,1)S(1)} %get-tuple-element.11), channel_id=1, source_target_pairs={{1,0},{3,2},{5,4},{7,6},{9,8},{11,10},{13,12},{15,14},{17,16},{19,... | collective-permute-start | bytes 294920 | tf_op jit(solution)/shard_map/ppermute | solution.py:24
  53.2 1.2 %constant_dynamic-slice_fusion = bf16[128,16,64]{2,1,0:T(8,128)(2,1)S(1)} fusion(bf16[128,16,128]{2,1,0:T(8,128)(2,1)} %bitcast.45, s32[]{:T(128)S(6)} %select_n.24), kind=kLoop, calls=%fused_computation.43 | loop fusion | bytes 524292 | tf_op jit(solution)/shard_map/dynamic_slice | solution.py:289
  54.5 1.3 %copy.22 = bf16[128,16,64]{0,1,2:T(8,128)(2,1)} copy(bf16[128,16,64]{2,1,0:T(8,128)(2,1)S(1)} %constant_dynamic-slice_fusion) | data formatting | bytes 524288
  55.8 1.1 %pad_maximum_fusion = bf16[152,16,256]{2,1,0:T(8,128)(2,1)S(1)} fusion(bf16[12,16,256]{2,1,0:T(8,128)(2,1)} %collective-permute-done.3, bf16[128,16,256]{2,1,0:T(8,128)(2,1)S(1)} %copy-done.1, bf16[12,16,256]{2,1,0:T(8,128)(2,1)} %collective-permute-done.2), kind=kLoop, calls=%fused_computation.20 | loop fusion | flops 1245184 | bytes 2490368 | tf_op jit(solution)/shard_map/concatenate | solution.py:20
  56.9 0.3 reshape.130
  57.2 3.1 %convolution_convert_fusion = bf16[2,16,128,128]{3,2,1,0:T(8,128)(2,1)} fusion(bf16[152,16,2,128]{3,2,1,0:T(2,128)(2,1)S(1)} %reshape.130, bf16[152,128]{1,0:T(8,128)(2,1)} %get-tuple-element.8, bf16[128,128]{1,0:T(8,128)(2,1)} %get-tuple-element.6), kind=kOutput, calls=%fused_computation.9 | convolution fusion | flops 294649856 | bytes 2365440 | tf_op jit(solution)/shard_map/dot_general | solution.py:286
  (23 shorter events, 0.1 us)
Async XLA Ops:
  0.6 1.8 %copy-start = (bf16[2,16,128,128]{3,2,1,0:T(8,128)(2,1)S(1)}, bf16[2,16,128,128]{3,2,1,0:T(8,128)(2,1)}, u32[]{:S(2)}) copy-start(bf16[2,16,128,128]{3,2,1,0:T(8,128)(2,1)} %param.9) | copy-start | bytes 3145732
  2.4 4.9 %copy-start.4 = (f32[1,3,65]{2,0,1:T(1,128)S(1)}, f32[1,3,65]{2,0,1:T(1,128)}, u32[]{:S(2)}) copy-start(f32[1,3,65]{2,0,1:T(1,128)} %param.16) | copy-start | bytes 2344
  2.4 4.9 %copy-start.6 = (s32[1,3]{1,0:T(1,128)S(1)}, s32[1,3]{1,0:T(1,128)}, u32[]{:S(2)}) copy-start(s32[1,3]{1,0:T(1,128)} %param.17) | copy-start | bytes 40
  2.4 5.2 %copy-start.5 = (f32[25]{0:T(128)S(1)}, f32[25]{0:T(128)}, u32[]{:S(2)}) copy-start(f32[25]{0:T(128)} %param.14) | copy-start | bytes 304
  2.4 6.3 %copy-start.3 = (s32[128,128]{1,0:T(8,128)S(1)}, s32[128,128]{1,0:T(8,128)}, u32[]{:S(2)}) copy-start(s32[128,128]{1,0:T(8,128)} %param.10) | copy-start | bytes 196612
  2.4 6.4 %copy-start.2 = (bf16[512,2,128]{2,1,0:T(2,128)(2,1)S(1)}, bf16[512,2,128]{2,1,0:T(2,128)(2,1)}, u32[]{:S(2)}) copy-start(bf16[512,2,128]{2,1,0:T(2,128)(2,1)} %param.13) | copy-start | bytes 786436
  2.9 7.5 %collective-permute-start = (bf16[2,16,12,128]{3,2,1,0:T(8,128)(2,1)S(1)}, bf16[2,16,12,128]{3,2,1,0:T(8,128)(2,1)S(1)}, u32[]{:S(2)}, u32[]{:S(2)}) collective-permute-start(bf16[2,16,12,128]{3,2,1,0:T(8,128)(2,1)S(1)} %get-tuple-element.12), channel_id=1, source_target_pairs={{0,1},{2,3},{4,5},{6,7},{8,9},{10,11},{12,13},{14,15},{16,17},{18,... | collective-permute-start | bytes 294920 | tf_op jit(solution)/shard_map/ppermute | solution.py:22
  4.2 6.2 %collective-permute-start.1 = (bf16[2,16,12,128]{3,2,1,0:T(8,128)(2,1)S(1)}, bf16[2,16,12,128]{3,2,1,0:T(8,128)(2,1)S(1)}, u32[]{:S(2)}, u32[]{:S(2)}) collective-permute-start(bf16[2,16,12,128]{3,2,1,0:T(8,128)(2,1)S(1)} %get-tuple-element.13), channel_id=1, source_target_pairs={{1,0},{3,2},{5,4},{7,6},{9,8},{11,10},{13,12},{15,14},{17,16},{19,... | collective-permute-start | bytes 294920 | tf_op jit(solution)/shard_map/ppermute | solution.py:24
  10.4 0.6 %copy-start.7 = (bf16[2,16,12,128]{3,2,1,0:T(8,128)(2,1)}, bf16[2,16,12,128]{3,2,1,0:T(8,128)(2,1)S(1)}, u32[]{:S(2)}) copy-start(bf16[2,16,12,128]{3,2,1,0:T(8,128)(2,1)S(1)} %collective-permute-done) | copy-start | bytes 294916
  11.1 0.7 %copy-start.8 = (bf16[2,16,12,128]{3,2,1,0:T(8,128)(2,1)}, bf16[2,16,12,128]{3,2,1,0:T(8,128)(2,1)S(1)}, u32[]{:S(2)}) copy-start(bf16[2,16,12,128]{3,2,1,0:T(8,128)(2,1)S(1)} %collective-permute-done.1) | copy-start | bytes 294916
  45.5 10.3 %copy-start.1 = (bf16[128,16,256]{2,1,0:T(8,128)(2,1)S(1)}, bf16[128,16,256]{2,1,0:T(8,128)(2,1)}, u32[]{:S(2)}) copy-start(bf16[128,16,256]{2,1,0:T(8,128)(2,1)} %get-tuple-element.5) | copy-start | bytes 3145732
  46.5 9.2 %collective-permute-start.2 = (bf16[12,16,256]{2,1,0:T(8,128)(2,1)S(1)}, bf16[12,16,256]{2,1,0:T(8,128)(2,1)}, u32[]{:S(2)}, u32[]{:S(2)}) collective-permute-start(bf16[12,16,256]{2,1,0:T(8,128)(2,1)S(1)} %get-tuple-element.10), channel_id=1, source_target_pairs={{0,1},{2,3},{4,5},{6,7},{8,9},{10,11},{12,13},{14,15},{16,17},{18,... | collective-permute-start | bytes 294920 | tf_op jit(solution)/shard_map/ppermute | solution.py:22
  47.8 8.0 %collective-permute-start.3 = (bf16[12,16,256]{2,1,0:T(8,128)(2,1)S(1)}, bf16[12,16,256]{2,1,0:T(8,128)(2,1)}, u32[]{:S(2)}, u32[]{:S(2)}) collective-permute-start(bf16[12,16,256]{2,1,0:T(8,128)(2,1)S(1)} %get-tuple-element.11), channel_id=1, source_target_pairs={{1,0},{3,2},{5,4},{7,6},{9,8},{11,10},{13,12},{15,14},{17,16},{19,... | collective-permute-start | bytes 294920 | tf_op jit(solution)/shard_map/ppermute | solution.py:24

commit v2 on v1

v2 whole, which is shorter than its diff:
```python
import functools

import jax
import jax.numpy as jnp
from jax import lax
from jax.experimental import pallas as pl
from jax.experimental.pallas import tpu as pltpu
from jax.sharding import PartitionSpec as P

MESH = pl.DeviceIdType.MESH
BF = jnp.bfloat16
F32 = jnp.float32


def banded(taps_ref, where_tap):
    out = jnp.zeros(where_tap.shape, F32)
    for k in range(taps_ref.shape[0]):
        out = jnp.where(where_tap == k, taps_ref[k], out)
    return out.astype(BF)


def lag_table(gain_ref, dil_ref, total):
    bands, taps = gain_ref.shape[1:]
    lag = lax.broadcasted_iota(jnp.int32, (1, 2 * total), 1) - (total - 1)
    row = jnp.zeros((1, 2 * total), F32)
    for b in range(bands):
        for k in range(taps):
            row = row + jnp.where(lag == dil_ref[0, b] * (k - (taps - 1) // 2), gain_ref[0, b, k], 0.0)
    spread = jnp.broadcast_to(row, (total, 2 * total))
    return pltpu.roll(spread, total + 1, 1, stride=1, stride_axis=0)[:, :total].astype(BF)


def kernel(
    movie_ref, sup_ref, own_ref, temp_ref, gain_ref, dil_ref, mask_ref, row_ref, col_ref,
    back_ref, tr_ref,
    hot, pall, part, xrecv, zsend, gath, lag_ref, lag_all, tbuf, tr_all, fold,
    spad, top_in, bot_in, top_res, bot_res, cells, tr_rows, tr_out,
    lag_s, lag_r, x1_s, x1_r, z1_s, z1_r, z2_s, z2_r, x2_s, x2_r, h_s, h_r,
):
    np_ = lax.axis_size("planes")
    nw = lax.axis_size("wide")
    nr = lax.axis_size("rep")
    p = lax.axis_index("planes")
    z = lax.axis_index("wide")
    r = lax.axis_index("rep")
    blocks, hb, frames, comps = part.shape
    planes_here, _, rows, width = movie_ref.shape
    rim = (row_ref.shape[0] - 1) // 2
    edge = (spad.shape[2] - rows) // 2
    images = planes_here * frames
    shapes = temp_ref.shape[0]
    tile = min(256, shapes)
    total = nw * frames
    step = 4

    barrier = pltpu.get_barrier_semaphore()

    @pl.when(r > 0)
    def _():
        pl.semaphore_signal(barrier, inc=1, device_id={"rep": r - 1}, device_id_type=MESH)

    @pl.when(r < nr - 1)
    def _():
        pl.semaphore_signal(barrier, inc=1, device_id={"rep": r + 1}, device_id_type=MESH)

    for k in range(1, nw):
        pl.semaphore_signal(barrier, inc=1, device_id={"wide": lax.rem(z + k, nw)}, device_id_type=MESH)
    for k in range(1, np_):
        pl.semaphore_signal(barrier, inc=1, device_id={"planes": lax.rem(p + k, np_)}, device_id_type=MESH)

    lag_ref[...] = lag_table(gain_ref, dil_ref, total)
    lag_all[z] = lag_ref[...]
    inner = lax.broadcasted_iota(jnp.int32, (width, width), 0)
    outer = lax.broadcasted_iota(jnp.int32, (width, width), 1)
    col_fwd = banded(col_ref, inner - outer + rim)

    pl.semaphore_wait(barrier, nw - 1 + np_ - 1 + lax.min(r, 1) + lax.min(nr - 1 - r, 1))

    def halo(source, lo, hi, top, bot, base):
        down = pltpu.make_async_remote_copy(
            src_ref=source.at[:, :, hi : hi + edge], dst_ref=top,
            send_sem=h_s.at[base], recv_sem=h_r.at[base],
            device_id={"rep": lax.min(r + 1, nr - 1)}, device_id_type=MESH)
        up = pltpu.make_async_remote_copy(
            src_ref=source.at[:, :, lo : lo + edge], dst_ref=bot,
            send_sem=h_s.at[base + 1], recv_sem=h_r.at[base + 1],
            device_id={"rep": lax.max(r - 1, 0)}, device_id_type=MESH)
        return down, up

    def halo_start(copies):
        @pl.when(r < nr - 1)
        def _():
            copies[0].start()

        @pl.when(r > 0)
        def _():
            copies[1].start()

    def halo_finish(copies, top, bot):
        @pl.when(r > 0)
        def _():
            copies[0].wait_recv()
            copies[1].wait_send()

        @pl.when(r == 0)
        def _():
            top[...] = jnp.zeros_like(top)

        @pl.when(r < nr - 1)
        def _():
            copies[1].wait_recv()
            copies[0].wait_send()

        @pl.when(r == nr - 1)
        def _():
            bot[...] = jnp.zeros_like(bot)

    in_copies = halo(movie_ref, 0, rows - edge, top_in, bot_in, 0)
    halo_start(in_copies)

    def to_wide(src, dst, send, recv, k):
        return pltpu.make_async_remote_copy(
            src_ref=src, dst_ref=dst, send_sem=send.at[k - 1], recv_sem=recv.at[k - 1],
            device_id={"wide": lax.rem(z + k, nw)}, device_id_type=MESH)

    def to_plane(src, dst, send, recv, dp, zi):
        slot = (dp - 1) * nw + zi
        return pltpu.make_async_remote_copy(
            src_ref=src, dst_ref=dst, send_sem=send.at[slot], recv_sem=recv.at[slot],
            device_id={"planes": lax.rem(p + dp, np_)}, device_id_type=MESH)

    def lag_copy(k):
        return to_wide(lag_ref, lag_all.at[z], lag_s, lag_r, k)

    def x1_copy(dp, zi):
        return to_plane(part.at[lax.rem(p + dp, np_) * nw + zi], xrecv.at[(dp - 1) * nw + zi], x1_s, x1_r, dp, zi)

    def z1_copy(k):
        return to_wide(zsend.at[lax.rem(z + k, nw)], gath.at[z], z1_s, z1_r, k)

    def z2_copy(k):
        return to_wide(tbuf.at[lax.rem(z + k, nw)], tr_all.at[p * nw + z], z2_s, z2_r, k)

    def x2_copy(dp, zi):
        return to_plane(tr_all.at[p * nw + zi], tr_all.at[p * nw + zi], x2_s, x2_r, dp, zi)

    for k in range(1, nw):
        lag_copy(k).start()

    def smooth(n, carry):
        for u in range(step):
            q = n * step + u
            pi, f = q // frames, lax.rem(q, frames)
            spad[pi, f, edge : edge + rows] = jnp.dot(
                movie_ref[pi, f], col_fwd, preferred_element_type=F32).astype(BF)
        return carry

    lax.fori_loop(0, images // step, smooth, 0)
    here = lax.broadcasted_iota(jnp.int32, (rows, rows + 2 * edge), 0)
    there = lax.broadcasted_iota(jnp.int32, (rows, rows + 2 * edge), 1) - edge
    row_fwd = banded(row_ref, there - here + rim)
    halo_finish(in_copies, top_in, bot_in)
    for pi in range(planes_here):
        for held, at in ((top_in, 0), (bot_in, edge + rows)):
            spad[pi, :, at : at + edge] = jnp.dot(
                held[pi].reshape(frames * edge, width), col_fwd, preferred_element_type=F32
            ).astype(BF).reshape(frames, edge, width)
    mask_all = mask_ref[...].reshape(rows, width).astype(F32)

    def along(n, carry):
        for u in range(step):
            q = n * step + u
            pi, f = q // frames, lax.rem(q, frames)
            value = jnp.dot(row_fwd, spad[pi, f], preferred_element_type=F32) * mask_all
            cells[pi, pl.ds(f, rows, stride=frames), :] = value
        return carry

    lax.fori_loop(0, images // step, along, 0)

    def block_cells(b):
        span = pl.ds(b * hb * frames, hb * frames)
        return jnp.concatenate([cells[pi, span, :] for pi in range(planes_here)], axis=1).astype(BF)

    ids = lax.broadcasted_iota(jnp.int32, (tile, comps), 0)

    def project(b):
        base = b * hb
        f_blk = block_cells(b)
        pall[...] = lax.dot_general(
            f_blk, temp_ref[...], (((1,), (1,)), ((), ())), preferred_element_type=F32).astype(BF)
        sup = sup_ref[b]
        for i in range(hb):
            row = sup[i : i + 1, :]
            for q in range(0, shapes, tile):
                hot[base + i, q : q + tile, :] = jnp.where(ids == row - q, 1.0, 0.0).astype(BF)
            part[b, i] = jnp.dot(
                pall[i * frames : (i + 1) * frames, :], hot[base + i], preferred_element_type=F32).astype(BF)

    def others(n, carry):
        dp = n // nw + 1
        zi = lax.rem(z + 1 + n, nw)
        project(lax.rem(p + dp, np_) * nw + zi)
        x1_copy(dp, zi).start()
        return carry

    lax.fori_loop(0, (np_ - 1) * nw, others, 0)

    def mine(n, carry):
        zi = lax.rem(z + 1 + n, nw)
        b = p * nw + zi
        project(b)
        acc = part[b].astype(F32)
        for dp in range(1, np_):
            x1_copy(dp, zi).wait_recv()
            acc = acc + xrecv[(dp - 1) * nw + zi].astype(F32)
        zsend[zi] = acc.astype(BF)

        @pl.when(n < nw - 1)
        def _():
            z1_copy(n + 1).start()

        return carry

    lax.fori_loop(0, nw, mine, 0)
    gath[z] = zsend[z]

    def arrived(k, carry):
        lag_copy(k).wait()
        z1_copy(k).wait()
        return carry

    lax.fori_loop(1, nw, arrived, 0)

    me = p * nw + z
    for i in range(hb):
        table = lag_all[own_ref[me * hb + i]]
        columns = gath[:, i].reshape(total, comps)
        scores = jnp.dot(table, columns, preferred_element_type=F32)
        tbuf[:, i] = jnp.maximum(scores, 0.0).astype(BF).reshape(nw, frames, comps)

    def give(k, carry):
        z2_copy(k).start()
        return carry

    lax.fori_loop(1, nw, give, 0)
    tr_all[me] = tbuf[z]

    def model(b):
        base = b * hb
        for i in range(hb):
            fold[i * frames : (i + 1) * frames, :] = lax.dot_general(
                tr_all[b, i], hot[base + i], (((1,), (1,)), ((), ())), preferred_element_type=F32).astype(BF)
        tr_rows[pl.ds(base * frames, hb * frames), :] = tr_all[b].reshape(hb * frames, comps).astype(F32)
        out = jnp.dot(fold[...], temp_ref[...], preferred_element_type=F32)
        mask = mask_ref[b].astype(F32)
        mask = jnp.broadcast_to(mask[:, None, :], (hb, frames, width)).reshape(hb * frames, width)
        mask = jnp.concatenate([mask] * planes_here, axis=1)
        left = (block_cells(b).astype(F32) - mask * out).astype(BF).astype(F32)
        for pi in range(planes_here):
            cells[pi, pl.ds(base * frames, hb * frames), :] = left[:, pi * width : (pi + 1) * width]

    def same_plane(k, carry):
        zi = lax.rem(z + nw - k, nw)

        @pl.when(k > 0)
        def _():
            z2_copy(lax.max(k, 1)).wait_recv()

        for dp in range(1, np_):
            x2_copy(dp, zi).start()
        model(p * nw + zi)
        return carry

    lax.fori_loop(0, nw, same_plane, 0)

    def other_planes(n, carry):
        dp = n // nw + 1
        zi = lax.rem(z + nw - lax.rem(n, nw), nw)
        x2_copy(dp, zi).wait_recv()
        model(lax.rem(p + np_ - dp, np_) * nw + zi)
        return carry

    lax.fori_loop(0, (np_ - 1) * nw, other_planes, 0)

    def edges(n, carry):
        for u in range(step):
            q = n * step + u
            pi, f = q // frames, lax.rem(q, frames)
            for at in (0, rows - edge):
                spad[pi, f, edge + at : 2 * edge + at] = cells[
                    pi, pl.ds(f + at * frames, edge, stride=frames), :].astype(BF)
        return carry

    lax.fori_loop(0, images // step, edges, 0)
    out_copies = halo(spad, edge, rows, top_res, bot_res, 2)
    halo_start(out_copies)

    def inside(n, carry):
        for u in range(step):
            q = n * step + u
            pi, f = q // frames, lax.rem(q, frames)
            spad[pi, f, 2 * edge : rows] = cells[
                pi, pl.ds(f + edge * frames, rows - 2 * edge, stride=frames), :].astype(BF)
        return carry

    lax.fori_loop(0, images // step, inside, 0)

    share = comps // np_
    pick = (
        lax.broadcasted_iota(jnp.int32, (share, comps), 0) + p * share
        == lax.broadcasted_iota(jnp.int32, (share, comps), 1)
    )
    pick = jnp.where(pick, 1.0, 0.0).astype(BF)
    for t in range(frames):
        one = tr_rows[pl.ds(t, rows, stride=frames), :].astype(BF)
        tr_out[pl.ds(t, share, stride=frames), :] = lax.dot_general(
            pick, one, (((1,), (1,)), ((), ())), preferred_element_type=F32)
    tr_ref[...] = tr_out[...].astype(BF).reshape(tr_ref.shape)

    row_adj = banded(row_ref, here - there + rim)
    col_adj = banded(col_ref, outer - inner + rim)
    halo_finish(out_copies, top_res, bot_res)
    spad[:, :, 0:edge] = top_res[...]
    spad[:, :, edge + rows :] = bot_res[...]

    def back(n, carry):
        for u in range(step):
            q = n * step + u
            pi, f = q // frames, lax.rem(q, frames)
            value = jnp.dot(row_adj, spad[pi, f], preferred_element_type=F32).astype(BF)
            back_ref[pi, f] = jnp.dot(value, col_adj, preferred_element_type=F32).astype(BF)
        return carry

    lax.fori_loop(0, images // step, back, 0)

    def drained_planes(n, carry):
        x1_copy(n // nw + 1, lax.rem(n, nw)).wait_send()
        x2_copy(n // nw + 1, lax.rem(n, nw)).wait_send()
        return carry

    lax.fori_loop(0, (np_ - 1) * nw, drained_planes, 0)

    def drained_wide(k, carry):
        z2_copy(k).wait_send()
        return carry

    lax.fori_loop(1, nw, drained_wide, 0)


def on_device(
    movie_frames, pixel_mask, tile_owner, support, templates, row_taps, col_taps, lag_gains, dilations
):
    np_ = lax.axis_size("planes")
    nw = lax.axis_size("wide")
    blocks = np_ * nw
    planes_here, frames, rows, width = movie_frames.shape
    hb = rows // blocks
    comps = support.shape[1]
    count = templates.shape[0]
    total = nw * frames
    rim = (row_taps.shape[0] - 1) // 2
    edge = -(-rim // 16) * 16
    shapes = templates.reshape(count, planes_here * width)
    vm = pl.BlockSpec(memory_space=pltpu.VMEM)
    sm = pl.BlockSpec(memory_space=pltpu.SMEM)
    dma = pltpu.SemaphoreType.DMA
    piece = (hb, frames, comps)
    across = (np_ - 1) * nw
    halo = pltpu.VMEM((planes_here, frames, edge, width), BF)
    back, traces = pl.pallas_call(
        kernel,
        out_shape=(
            jax.ShapeDtypeStruct(movie_frames.shape, BF),
            jax.ShapeDtypeStruct((comps // np_, frames, rows), BF),
        ),
        in_specs=[vm, vm, sm, vm, sm, sm, vm, sm, sm],
        out_specs=(vm, vm),
        scratch_shapes=[
            pltpu.VMEM((rows, count, comps), BF),
            pltpu.VMEM((hb * frames, count), BF),
            pltpu.VMEM((blocks,) + piece, BF),
            pltpu.VMEM((across,) + piece, BF),
            pltpu.VMEM((nw,) + piece, BF),
            pltpu.VMEM((nw,) + piece, BF),
            pltpu.VMEM((total, total), BF),
            pltpu.VMEM((nw, total, total), BF),
            pltpu.VMEM((nw,) + piece, BF),
            pltpu.VMEM((blocks,) + piece, BF),
            pltpu.VMEM((hb * frames, count), BF),
            pltpu.VMEM((planes_here, frames, rows + 2 * edge, width), BF),
            halo, halo, halo, halo,
            pltpu.VMEM((planes_here, rows * frames, width), F32),
            pltpu.VMEM((rows * frames, comps), F32),
            pltpu.VMEM((comps // np_ * frames, rows), F32),
            dma((nw - 1,)), dma((nw - 1,)),
            dma((across,)), dma((across,)),
            dma((nw - 1,)), dma((nw - 1,)),
            dma((nw - 1,)), dma((nw - 1,)),
            dma((across,)), dma((across,)),
            dma((4,)), dma((4,)),
        ],
        compiler_params=pltpu.CompilerParams(
            collective_id=0, has_side_effects=True, vmem_limit_bytes=63 * 1024 * 1024
        ),
    )(
        movie_frames,
        support.reshape(blocks, hb, comps),
        tile_owner[:, 0],
        shapes,
        lag_gains,
        dilations,
        pixel_mask.reshape(blocks, hb, width),
        row_taps,
        col_taps,
    )
    return (traces, back)


def solution(mesh):
    return jax.shard_map(
        on_device,
        mesh=mesh,
        in_specs=(
            P("planes", ("groups", "wide"), "rep", None),
            P("rep", None),
            P("rep", None),
            P("rep", None),
            P(None, "planes", None),
            P(),
            P(),
            P("wide", None, None),
            P("wide", None),
        ),
        out_specs=(
            P("planes", ("groups", "wide"), "rep"),
            P("planes", ("groups", "wide"), "rep", None),
        ),
        check_vma=False,
    )
```

time: 60.7 us -> 49.8 us (0.82)
  the two profiles are of different devices: /device:TPU:1 before, /device:TPU:0 now
where the time goes in v2:
time: 49.8 us; the launch traced here: 49.6 us
  Pallas kernels  42 us (84%)
  local copies, waits for them, and re-layouts  6.91 us (14%)
  between operations  0.65 us (1%)
    pallas_call x1, Pallas kernels, on_device(): pl.pallas_call(kernel, out_shape=(jax.ShapeDtypeStruct(movie_frames.shape...  42 us
    unnamed x6, local copies, waits for them, and re-layouts  6.91 us

profile of v2, /device:TPU:0, one launch (start us, length us, event | category | flops | bytes accessed | tf_op | source)
XLA Modules:
  0.0 49.6 jit_solution(8041606957203411735)
XLA Ops:
  0.6 0.0 copy-start
  0.6 0.7 %copy-done = f32[1,3,65]{2,0,1:T(1,128)S(1)} copy-done((f32[1,3,65]{2,0,1:T(1,128)S(1)}, f32[1,3,65]{2,0,1:T(1,128)}, u32[]{:S(2)}) %copy-start) | copy-done | bytes 804
  1.3 0.6 %copy.11.gain_ref = f32[1,3,65]{2,1,0:T(4,128)} copy(f32[1,3,65]{2,0,1:T(1,128)S(1)} %copy-done) | data formatting | bytes 1560 | tf_op args[7]
  1.9 1.7 %copy.14 = bf16[64,8,2,128]{3,1,2,0:T(8,128)(2,1)} copy(bf16[64,8,2,128]{3,2,1,0:T(2,128)(2,1)} %bitcast.8) | data formatting | bytes 524288
  3.6 42.0 %shard_map.104 = (bf16[2,16,128,128]{3,2,1,0:T(8,128)(2,1)}, bf16[64,16,128]{2,1,0:T(8,128)(2,1)}) custom-call(bf16[2,16,128,128]{3,2,1,0:T(8,128)(2,1)} %movie_ref.1, s32[8,16,128]{2,1,0:T(8,128)} %bitcast.9, s32[128]{0:T(128)} %bitcast.11, bf16[512,256]{1,0:T(8,128)(2,1)} %bitcast.7, f32[1,3,65]{2,1,0:T(4,128)} %copy.11.gain_ref, s32[1,3]{1,0:T(1,128)} %dil_ref.1, ...), custom_call_target="tpu_custom_call" | custom-call | tf_op jit(solution)/shard_map/pallas_call | solution.py:370
  45.6 1.7 %copy.17 = bf16[64,16,128]{2,1,0:T(8,128)(2,1)} copy(bf16[64,16,128]{2,1,0:T(8,128)(2,1)} %get-tuple-element.8) | data formatting | bytes 524288
  47.3 2.3 %copy.18 = bf16[2,16,128,128]{3,2,1,0:T(8,128)(2,1)} copy(bf16[2,16,128,128]{3,2,1,0:T(8,128)(2,1)} %get-tuple-element.9) | data formatting | bytes 2097152
Async XLA Ops:
  0.6 0.7 %copy-start = (f32[1,3,65]{2,0,1:T(1,128)S(1)}, f32[1,3,65]{2,0,1:T(1,128)}, u32[]{:S(2)}) copy-start(f32[1,3,65]{2,0,1:T(1,128)} %param.16) | copy-start | bytes 2344

commit v3 on v2

--- a/solution.py
+++ b/solution.py
@@ -20,21 +20,21 @@
 
 
 def lag_table(gain_ref, dil_ref, total):
-    bands, taps = gain_ref.shape[1:]
+    bands, _, taps = gain_ref.shape
     lag = lax.broadcasted_iota(jnp.int32, (1, 2 * total), 1) - (total - 1)
     row = jnp.zeros((1, 2 * total), F32)
     for b in range(bands):
         for k in range(taps):
-            row = row + jnp.where(lag == dil_ref[0, b] * (k - (taps - 1) // 2), gain_ref[0, b, k], 0.0)
+            row = row + jnp.where(lag == dil_ref[0, b] * (k - (taps - 1) // 2), gain_ref[b, 0, k], 0.0)
     spread = jnp.broadcast_to(row, (total, 2 * total))
     return pltpu.roll(spread, total + 1, 1, stride=1, stride_axis=0)[:, :total].astype(BF)
 
 
 def kernel(
-    movie_ref, sup_ref, own_ref, temp_ref, gain_ref, dil_ref, mask_ref, row_ref, col_ref,
-    back_ref, tr_ref,
-    hot, pall, part, xrecv, zsend, gath, lag_ref, lag_all, tbuf, tr_all, fold,
-    spad, top_in, bot_in, top_res, bot_res, cells, tr_rows, tr_out,
+    movie_ref, sup_ref, own_ref, table_ref, gain_ref, dil_ref, mask_ref, row_ref, col_ref,
+    spad, tr_ref,
+    temp_ref, hot, pall, part, xrecv, zsend, gath, lag_ref, lag_all, tbuf, tr_all, fold,
+    top_in, bot_in, top_res, bot_res, cells, tr_rows, tr_out,
     lag_s, lag_r, x1_s, x1_r, z1_s, z1_r, z2_s, z2_r, x2_s, x2_r, h_s, h_r,
 ):
     np_ = lax.axis_size("planes")
@@ -70,6 +70,8 @@
 
     lag_ref[...] = lag_table(gain_ref, dil_ref, total)
     lag_all[z] = lag_ref[...]
+    for pi in range(planes_here):
+        temp_ref[:, pi * width : (pi + 1) * width] = table_ref[:, pi, :]
     inner = lax.broadcasted_iota(jnp.int32, (width, width), 0)
     outer = lax.broadcasted_iota(jnp.int32, (width, width), 1)
     col_fwd = banded(col_ref, inner - outer + rim)
@@ -317,21 +319,10 @@
             pick, one, (((1,), (1,)), ((), ())), preferred_element_type=F32)
     tr_ref[...] = tr_out[...].astype(BF).reshape(tr_ref.shape)
 
-    row_adj = banded(row_ref, here - there + rim)
-    col_adj = banded(col_ref, outer - inner + rim)
     halo_finish(out_copies, top_res, bot_res)
     spad[:, :, 0:edge] = top_res[...]
     spad[:, :, edge + rows :] = bot_res[...]
 
-    def back(n, carry):
-        for u in range(step):
-            q = n * step + u
-            pi, f = q // frames, lax.rem(q, frames)
-            value = jnp.dot(row_adj, spad[pi, f], preferred_element_type=F32).astype(BF)
-            back_ref[pi, f] = jnp.dot(value, col_adj, preferred_element_type=F32).astype(BF)
-        return carry
-
-    lax.fori_loop(0, images // step, back, 0)
 
     def drained_planes(n, carry):
         x1_copy(n // nw + 1, lax.rem(n, nw)).wait_send()
@@ -345,6 +336,24 @@
         return carry
 
     lax.fori_loop(1, nw, drained_wide, 0)
+
+
+def adjoint_kernel(rim, edge, pad_ref, tr_ref, row_ref, col_ref, back_ref, out_ref, row_adj, col_adj):
+    rows, width = back_ref.shape[1:]
+
+    @pl.when(pl.program_id(0) == 0)
+    def _():
+        here = lax.broadcasted_iota(jnp.int32, row_adj.shape, 0)
+        there = lax.broadcasted_iota(jnp.int32, row_adj.shape, 1) - edge
+        row_adj[...] = banded(row_ref, here - there + rim)
+        inner = lax.broadcasted_iota(jnp.int32, (width, width), 0)
+        outer = lax.broadcasted_iota(jnp.int32, (width, width), 1)
+        col_adj[...] = banded(col_ref, outer - inner + rim)
+
+    for q in range(back_ref.shape[0]):
+        value = jnp.dot(row_adj[...], pad_ref[q], preferred_element_type=F32).astype(BF)
+        back_ref[q] = jnp.dot(value, col_adj[...], preferred_element_type=F32).astype(BF)
+    out_ref[...] = tr_ref[...]
 
 
 def on_device(
@@ -360,22 +369,23 @@
     total = nw * frames
     rim = (row_taps.shape[0] - 1) // 2
     edge = -(-rim // 16) * 16
-    shapes = templates.reshape(count, planes_here * width)
     vm = pl.BlockSpec(memory_space=pltpu.VMEM)
     sm = pl.BlockSpec(memory_space=pltpu.SMEM)
     dma = pltpu.SemaphoreType.DMA
     piece = (hb, frames, comps)
     across = (np_ - 1) * nw
     halo = pltpu.VMEM((planes_here, frames, edge, width), BF)
-    back, traces = pl.pallas_call(
+    padded = (planes_here * frames, rows + 2 * edge, width)
+    held, traces = pl.pallas_call(
         kernel,
         out_shape=(
-            jax.ShapeDtypeStruct(movie_frames.shape, BF),
+            jax.ShapeDtypeStruct((planes_here, frames) + padded[1:], BF),
             jax.ShapeDtypeStruct((comps // np_, frames, rows), BF),
         ),
         in_specs=[vm, vm, sm, vm, sm, sm, vm, sm, sm],
         out_specs=(vm, vm),
         scratch_shapes=[
+            pltpu.VMEM((count, planes_here * width), BF),
             pltpu.VMEM((rows, count, comps), BF),
             pltpu.VMEM((hb * frames, count), BF),
             pltpu.VMEM((blocks,) + piece, BF),
@@ -387,7 +397,6 @@
             pltpu.VMEM((nw,) + piece, BF),
             pltpu.VMEM((blocks,) + piece, BF),
             pltpu.VMEM((hb * frames, count), BF),
-            pltpu.VMEM((planes_here, frames, rows + 2 * edge, width), BF),
             halo, halo, halo, halo,
             pltpu.VMEM((planes_here, rows * frames, width), F32),
             pltpu.VMEM((rows * frames, comps), F32),
@@ -400,20 +409,41 @@
             dma((4,)), dma((4,)),
         ],
         compiler_params=pltpu.CompilerParams(
-            collective_id=0, has_side_effects=True, vmem_limit_bytes=63 * 1024 * 1024
+            collective_id=0, has_side_effects=True, vmem_limit_bytes=2 * (rows * count * comps + nw * total * total) + 24 * 1024 * 1024
         ),
     )(
         movie_frames,
         support.reshape(blocks, hb, comps),
         tile_owner[:, 0],
-        shapes,
-        lag_gains,
+        templates,
+        jnp.transpose(lag_gains, (1, 0, 2)),
         dilations,
         pixel_mask.reshape(blocks, hb, width),
         row_taps,
         col_taps,
     )
-    return (traces, back)
+    steps = frames // 2
+    few = padded[0] // steps
+    share = traces.shape[0] // steps if traces.shape[0] % steps == 0 else 0
+    part_spec = pl.BlockSpec((share,) + traces.shape[1:], lambda i: (i, 0, 0))
+    back, traces = pl.pallas_call(
+        functools.partial(adjoint_kernel, rim, edge),
+        grid=(steps,),
+        out_shape=(
+            jax.ShapeDtypeStruct((padded[0], rows, width), BF),
+            jax.ShapeDtypeStruct(traces.shape, BF),
+        ),
+        in_specs=[
+            pl.BlockSpec((few,) + padded[1:], lambda i: (i, 0, 0)),
+            part_spec,
+            sm,
+            sm,
+        ],
+        out_specs=(pl.BlockSpec((few, rows, width), lambda i: (i, 0, 0)), part_spec),
+        scratch_shapes=[pltpu.VMEM((rows, rows + 2 * edge), BF), pltpu.VMEM((width, width), BF)],
+        compiler_params=pltpu.CompilerParams(vmem_limit_bytes=16 * 1024 * 1024),
+    )(held.reshape(padded), traces, row_taps, col_taps)
+    return (traces, back.reshape(movie_frames.shape))
 
 
 def solution(mesh):

time: 49.8 us -> 50.5 us (1.014)
    pallas_call x1 -> x2, Pallas kernels: 42 us -> 42.4 us  [the longest x1 35.7 us: on_device(): pl.pallas_call(kernel, out_shape=(jax.ShapeDtypeStruct((planes_here, fram...]
    unnamed x6 -> x18, local copies, waits for them, and re-layouts: 6.91 us -> 7.14 us
where the time goes in v3:
time: 50.5 us; the launch traced here: 50.2 us
  Pallas kernels  42.4 us (84%)
  local copies, waits for them, and re-layouts  7.14 us (14%)
  between operations  0.66 us (1%)
    pallas_call x1, Pallas kernels, on_device(): pl.pallas_call(kernel, out_shape=(jax.ShapeDtypeStruct((planes_here, fram...  35.7 us
    unnamed x18, local copies, waits for them, and re-layouts  7.14 us
    pallas_call x1, Pallas kernels, on_device(): pl.pallas_call(functools.partial(adjoint_kernel, rim, edge), grid=(steps,...  6.69 us

profile of v3, /device:TPU:0, one launch (start us, length us, event | category | flops | bytes accessed | tf_op | source)
XLA Modules:
  0.0 50.2 jit_solution(14999200494880404803)
XLA Ops:
  0.6 0.0 copy-start
  0.6 1.2 %copy-done = bf16[2,16,128,128]{3,2,1,0:T(8,128)(2,1)S(1)} copy-done((bf16[2,16,128,128]{3,2,1,0:T(8,128)(2,1)S(1)}, bf16[2,16,128,128]{3,2,1,0:T(8,128)(2,1)}, u32[]{:S(2)}) %copy-start) | copy-done | bytes 1048600
  1.9 0.0 copy-start.1
  1.9 0.9 %copy-done.1 = bf16[512,2,128]{2,1,0:T(2,128)(2,1)S(1)} copy-done((bf16[512,2,128]{2,1,0:T(2,128)(2,1)S(1)}, bf16[512,2,128]{2,1,0:T(2,128)(2,1)}, u32[]{:S(2)}) %copy-start.1) | copy-done | bytes 262168
  2.8 0.0 copy-start.2
  2.8 0.8 %copy-done.2 = s32[128,128]{1,0:T(8,128)S(1)} copy-done((s32[128,128]{1,0:T(8,128)S(1)}, s32[128,128]{1,0:T(8,128)}, u32[]{:S(2)}) %copy-start.2) | copy-done | bytes 65560
  3.6 0.0 copy-start.3
  3.7 0.8 %copy-done.3 = s32[128,128]{1,0:T(8,128)S(1)} copy-done((s32[128,128]{1,0:T(8,128)S(1)}, s32[128,128]{1,0:T(8,128)}, u32[]{:S(2)}) %copy-start.3) | copy-done | bytes 65560
  4.5 0.0 copy-start.4
  4.5 0.7 %copy-done.4 = f32[25]{0:T(128)S(1)} copy-done((f32[25]{0:T(128)S(1)}, f32[25]{0:T(128)}, u32[]{:S(2)}) %copy-start.4) | copy-done | bytes 124
  5.1 0.0 copy-start.5
  5.1 0.7 %copy-done.5 = f32[25]{0:T(128)S(1)} copy-done((f32[25]{0:T(128)S(1)}, f32[25]{0:T(128)}, u32[]{:S(2)}) %copy-start.5) | copy-done | bytes 124
  5.8 0.0 copy-start.6
  5.8 0.7 %copy-done.6 = f32[1,3,65]{2,0,1:T(1,128)S(1)} copy-done((f32[1,3,65]{2,0,1:T(1,128)S(1)}, f32[1,3,65]{2,0,1:T(1,128)}, u32[]{:S(2)}) %copy-start.6) | copy-done | bytes 804
  6.5 0.0 copy-start.7
  6.5 0.7 %copy-done.7 = s32[128,1]{0,1:T(1,128)S(1)} copy-done((s32[128,1]{0,1:T(1,128)S(1)}, s32[128,1]{0,1:T(1,128)}, u32[]{:S(2)}) %copy-start.7) | copy-done | bytes 536
  7.1 0.0 copy-start.8
  7.1 0.7 %copy-done.8 = s32[1,3]{1,0:T(1,128)S(1)} copy-done((s32[1,3]{1,0:T(1,128)S(1)}, s32[1,3]{1,0:T(1,128)}, u32[]{:S(2)}) %copy-start.8) | copy-done | bytes 36
  7.8 35.7 %shard_map.104 = (bf16[2,16,160,128]{3,2,1,0:T(8,128)(2,1)S(1)}, bf16[64,16,128]{2,1,0:T(8,128)(2,1)S(1)}) custom-call(bf16[2,16,128,128]{3,2,1,0:T(8,128)(2,1)S(1)} %copy-done, s32[8,16,128]{2,1,0:T(8,128)S(1)} %bitcast.7, s32[128]{0:T(128)S(1)} %bitcast.10, bf16[512,2,128]{2,1,0:T(2,128)(2,1)S(1)} %copy-done.1, f32[3,1,65]{2,1,0:T(1,128)S(1)} %bitcast.9, ...), custom_call_target="tpu_custom_call" | custom-call | tf_op jit(solution)/shard_map/pallas_call | solution.py:379
  43.5 6.7 %shard_map.105 = (bf16[32,128,128]{2,1,0:T(8,128)(2,1)}, bf16[64,16,128]{2,1,0:T(8,128)(2,1)}) custom-call(bf16[32,160,128]{2,1,0:T(8,128)(2,1)S(1)} %bitcast.6, bf16[64,16,128]{2,1,0:T(8,128)(2,1)S(1)} %get-tuple-element.7.tr_ref, f32[25]{0:T(128)S(1)} %copy-done.4, f32[25]{0:T(128)S(1)} %copy-done.5), custom_call_target="tpu_custom_call" | custom-call | tf_op jit(solution)/shard_map/pallas_call | solution.py:429
Async XLA Ops:
  0.6 1.2 %copy-start = (bf16[2,16,128,128]{3,2,1,0:T(8,128)(2,1)S(1)}, bf16[2,16,128,128]{3,2,1,0:T(8,128)(2,1)}, u32[]{:S(2)}) copy-start(bf16[2,16,128,128]{3,2,1,0:T(8,128)(2,1)} %movie_ref.1) | copy-start | bytes 3145732
  1.9 0.9 %copy-start.1 = (bf16[512,2,128]{2,1,0:T(2,128)(2,1)S(1)}, bf16[512,2,128]{2,1,0:T(2,128)(2,1)}, u32[]{:S(2)}) copy-start(bf16[512,2,128]{2,1,0:T(2,128)(2,1)} %table_ref.1) | copy-start | bytes 786436
  2.8 0.8 %copy-start.2 = (s32[128,128]{1,0:T(8,128)S(1)}, s32[128,128]{1,0:T(8,128)}, u32[]{:S(2)}) copy-start(s32[128,128]{1,0:T(8,128)} %param.12) | copy-start | bytes 196612
  3.6 0.8 %copy-start.3 = (s32[128,128]{1,0:T(8,128)S(1)}, s32[128,128]{1,0:T(8,128)}, u32[]{:S(2)}) copy-start(s32[128,128]{1,0:T(8,128)} %param.10) | copy-start | bytes 196612
  4.5 0.7 %copy-start.4 = (f32[25]{0:T(128)S(1)}, f32[25]{0:T(128)}, u32[]{:S(2)}) copy-start(f32[25]{0:T(128)} %row_ref.3) | copy-start | bytes 304
  5.1 0.7 %copy-start.5 = (f32[25]{0:T(128)S(1)}, f32[25]{0:T(128)}, u32[]{:S(2)}) copy-start(f32[25]{0:T(128)} %col_ref.3) | copy-start | bytes 304
  5.8 0.7 %copy-start.6 = (f32[1,3,65]{2,0,1:T(1,128)S(1)}, f32[1,3,65]{2,0,1:T(1,128)}, u32[]{:S(2)}) copy-start(f32[1,3,65]{2,0,1:T(1,128)} %param.16) | copy-start | bytes 2344
  6.5 0.7 %copy-start.7 = (s32[128,1]{0,1:T(1,128)S(1)}, s32[128,1]{0,1:T(1,128)}, u32[]{:S(2)}) copy-start(s32[128,1]{0,1:T(1,128)} %param.11) | copy-start | bytes 1540
  7.1 0.7 %copy-start.8 = (s32[1,3]{1,0:T(1,128)S(1)}, s32[1,3]{1,0:T(1,128)}, u32[]{:S(2)}) copy-start(s32[1,3]{1,0:T(1,128)} %dil_ref.1) | copy-start | bytes 40

commit v4 on v3

--- a/solution.py
+++ b/solution.py
@@ -52,6 +52,7 @@
     tile = min(256, shapes)
     total = nw * frames
     step = 4
+    many = 8
 
     barrier = pltpu.get_barrier_semaphore()
 
@@ -150,14 +151,13 @@
         lag_copy(k).start()
 
     def smooth(n, carry):
-        for u in range(step):
-            q = n * step + u
-            pi, f = q // frames, lax.rem(q, frames)
-            spad[pi, f, edge : edge + rows] = jnp.dot(
-                movie_ref[pi, f], col_fwd, preferred_element_type=F32).astype(BF)
-        return carry
-
-    lax.fori_loop(0, images // step, smooth, 0)
+        pi, f = n * many // frames, lax.rem(n * many, frames)
+        spad[pi, pl.ds(f, many), edge : edge + rows] = jnp.dot(
+            movie_ref[pi, pl.ds(f, many)].reshape(many * rows, width), col_fwd, preferred_element_type=F32
+        ).astype(BF).reshape(many, rows, width)
+        return carry
+
+    lax.fori_loop(0, images // many, smooth, 0)
     here = lax.broadcasted_iota(jnp.int32, (rows, rows + 2 * edge), 0)
     there = lax.broadcasted_iota(jnp.int32, (rows, rows + 2 * edge), 1) - edge
     row_fwd = banded(row_ref, there - here + rim)
@@ -170,14 +170,17 @@
     mask_all = mask_ref[...].reshape(rows, width).astype(F32)
 
     def along(n, carry):
-        for u in range(step):
-            q = n * step + u
+        for u in range(0, many, 2):
+            q = n * many + u
             pi, f = q // frames, lax.rem(q, frames)
-            value = jnp.dot(row_fwd, spad[pi, f], preferred_element_type=F32) * mask_all
-            cells[pi, pl.ds(f, rows, stride=frames), :] = value
-        return carry
-
-    lax.fori_loop(0, images // step, along, 0)
+            pair = jnp.concatenate([spad[pi, f], spad[pi, f + 1]], axis=1)
+            value = jnp.dot(row_fwd, pair, preferred_element_type=F32)
+            for v in range(2):
+                cells[pi, pl.ds(f + v, rows, stride=frames), :] = (
+                    value[:, v * width : (v + 1) * width] * mask_all)
+        return carry
+
+    lax.fori_loop(0, images // many, along, 0)
 
     def block_cells(b):
         span = pl.ds(b * hb * frames, hb * frames)
@@ -350,9 +353,15 @@
         outer = lax.broadcasted_iota(jnp.int32, (width, width), 1)
         col_adj[...] = banded(col_ref, outer - inner + rim)
 
-    for q in range(back_ref.shape[0]):
-        value = jnp.dot(row_adj[...], pad_ref[q], preferred_element_type=F32).astype(BF)
-        back_ref[q] = jnp.dot(value, col_adj[...], preferred_element_type=F32).astype(BF)
+    count = back_ref.shape[0]
+    parts = []
+    for q in range(0, count, 2):
+        pair = jnp.concatenate([pad_ref[q], pad_ref[q + 1]], axis=1)
+        value = jnp.dot(row_adj[...], pair, preferred_element_type=F32).astype(BF)
+        parts += [value[:, :width], value[:, width:]]
+    back_ref[...] = jnp.dot(
+        jnp.concatenate(parts, axis=0), col_adj[...], preferred_element_type=F32
+    ).astype(BF).reshape(count, rows, width)
     out_ref[...] = tr_ref[...]
 
 
@@ -409,7 +418,7 @@
             dma((4,)), dma((4,)),
         ],
         compiler_params=pltpu.CompilerParams(
-            collective_id=0, has_side_effects=True, vmem_limit_bytes=2 * (rows * count * comps + nw * total * total) + 24 * 1024 * 1024
+            collective_id=0, has_side_effects=True, vmem_limit_bytes=63 * 1024 * 1024
         ),
     )(
         movie_frames,
@@ -422,7 +431,7 @@
         row_taps,
         col_taps,
     )
-    steps = frames // 2
+    steps = frames // 4
     few = padded[0] // steps
     share = traces.shape[0] // steps if traces.shape[0] % steps == 0 else 0
     part_spec = pl.BlockSpec((share,) + traces.shape[1:], lambda i: (i, 0, 0))
@@ -441,7 +450,7 @@
         ],
         out_specs=(pl.BlockSpec((few, rows, width), lambda i: (i, 0, 0)), part_spec),
         scratch_shapes=[pltpu.VMEM((rows, rows + 2 * edge), BF), pltpu.VMEM((width, width), BF)],
-        compiler_params=pltpu.CompilerParams(vmem_limit_bytes=16 * 1024 * 1024),
+        compiler_params=pltpu.CompilerParams(vmem_limit_bytes=63 * 1024 * 1024),
     )(held.reshape(padded), traces, row_taps, col_taps)
     return (traces, back.reshape(movie_frames.shape))
 

time: 50.5 us -> 41.3 us (0.82)
  local copies, waits for them, and re-layouts: 7.14 us -> 0 us
  Pallas kernels: 42.4 us -> 40.4 us
    unnamed x18 -> x0, local copies, waits for them, and re-layouts: 7.14 us -> none
    pallas_call x1, Pallas kernels: 6.69 us -> 4.55 us  [on_device(): pl.pallas_call(functools.partial(adjoint_kernel, rim, edge), grid=(steps,...]
where the time goes in v4:
time: 41.3 us; the launch traced here: 41.1 us
  Pallas kernels  40.4 us (98%)
  between operations  0.64 us (2%)
    pallas_call x1, Pallas kernels, on_device(): pl.pallas_call(kernel, out_shape=(jax.ShapeDtypeStruct((planes_here, fram...  35.9 us
    pallas_call x1, Pallas kernels, on_device(): pl.pallas_call(functools.partial(adjoint_kernel, rim, edge), grid=(steps,...  4.55 us

profile of v4, /device:TPU:0, one launch (start us, length us, event | category | flops | bytes accessed | tf_op | source)
XLA Modules:
  0.0 41.1 jit_solution(7501311324161248906)
XLA Ops:
  0.6 35.9 %shard_map.104 = (bf16[2,16,160,128]{3,2,1,0:T(8,128)(2,1)}, bf16[64,16,128]{2,1,0:T(8,128)(2,1)}) custom-call(bf16[2,16,128,128]{3,2,1,0:T(8,128)(2,1)} %movie_ref.1, s32[8,16,128]{2,1,0:T(8,128)} %bitcast.7, s32[128]{0:T(128)} %bitcast.10, bf16[512,2,128]{2,1,0:T(2,128)(2,1)} %table_ref.1, f32[3,1,65]{2,1,0:T(1,128)} %bitcast.9, s32[1,3]{1,0:T(1,128)} %dil_ref.1, ...), custom_call_target="tpu_custom_call" | custom-call | tf_op jit(solution)/shard_map/pallas_call | solution.py:388
  36.5 4.6 %shard_map.105 = (bf16[32,128,128]{2,1,0:T(8,128)(2,1)}, bf16[64,16,128]{2,1,0:T(8,128)(2,1)}) custom-call(bf16[32,160,128]{2,1,0:T(8,128)(2,1)} %bitcast.6, bf16[64,16,128]{2,1,0:T(8,128)(2,1)} %get-tuple-element.7.tr_ref, f32[25]{0:T(128)} %row_ref.3, f32[25]{0:T(128)} %col_ref.3), custom_call_target="tpu_custom_call" | custom-call | tf_op jit(solution)/shard_map/pallas_call | solution.py:438

commit v5 on v4

--- a/solution.py
+++ b/solution.py
@@ -71,8 +71,6 @@
 
     lag_ref[...] = lag_table(gain_ref, dil_ref, total)
     lag_all[z] = lag_ref[...]
-    for pi in range(planes_here):
-        temp_ref[:, pi * width : (pi + 1) * width] = table_ref[:, pi, :]
     inner = lax.broadcasted_iota(jnp.int32, (width, width), 0)
     outer = lax.broadcasted_iota(jnp.int32, (width, width), 1)
     col_fwd = banded(col_ref, inner - outer + rim)
@@ -120,6 +118,8 @@
 
     in_copies = halo(movie_ref, 0, rows - edge, top_in, bot_in, 0)
     halo_start(in_copies)
+    for pi in range(planes_here):
+        temp_ref[:, pi * width : (pi + 1) * width] = table_ref[:, pi, :]
 
     def to_wide(src, dst, send, recv, k):
         return pltpu.make_async_remote_copy(
@@ -186,7 +186,8 @@
         span = pl.ds(b * hb * frames, hb * frames)
         return jnp.concatenate([cells[pi, span, :] for pi in range(planes_here)], axis=1).astype(BF)
 
-    ids = lax.broadcasted_iota(jnp.int32, (tile, comps), 0)
+    ids = lax.broadcasted_iota(jnp.int32, (tile, comps), 0).astype(F32).astype(BF)
+    one, none = jnp.ones((), BF), jnp.zeros((), BF)
 
     def project(b):
         base = b * hb
@@ -196,10 +197,16 @@
         sup = sup_ref[b]
         for i in range(hb):
             row = sup[i : i + 1, :]
-            for q in range(0, shapes, tile):
-                hot[base + i, q : q + tile, :] = jnp.where(ids == row - q, 1.0, 0.0).astype(BF)
+            marks = jnp.concatenate(
+                [
+                    jnp.where(ids == (row - q).astype(F32).astype(BF), one, none)
+                    for q in range(0, shapes, tile)
+                ],
+                axis=0,
+            )
+            hot[base + i] = marks
             part[b, i] = jnp.dot(
-                pall[i * frames : (i + 1) * frames, :], hot[base + i], preferred_element_type=F32).astype(BF)
+                pall[i * frames : (i + 1) * frames, :], marks, preferred_element_type=F32).astype(BF)
 
     def others(n, carry):
         dp = n // nw + 1

time: 41.3 us -> 41 us (level)
  no operation moved by 1% of the time
where the time goes in v5:
time: 41 us; the launch traced here: 40.8 us
  Pallas kernels  40.2 us (98%)
  between operations  0.64 us (2%)
    pallas_call x1, Pallas kernels, on_device(): pl.pallas_call(kernel, out_shape=(jax.ShapeDtypeStruct((planes_here, fram...  35.6 us
    pallas_call x1, Pallas kernels, on_device(): pl.pallas_call(functools.partial(adjoint_kernel, rim, edge), grid=(steps,...  4.56 us

profile of v5, /device:TPU:0, one launch (start us, length us, event | category | flops | bytes accessed | tf_op | source)
XLA Modules:
  0.0 40.8 jit_solution(16488008384251773461)
XLA Ops:
  0.6 35.6 %shard_map.104 = (bf16[2,16,160,128]{3,2,1,0:T(8,128)(2,1)}, bf16[64,16,128]{2,1,0:T(8,128)(2,1)}) custom-call(bf16[2,16,128,128]{3,2,1,0:T(8,128)(2,1)} %movie_ref.1, s32[8,16,128]{2,1,0:T(8,128)} %bitcast.7, s32[128]{0:T(128)} %bitcast.10, bf16[512,2,128]{2,1,0:T(2,128)(2,1)} %table_ref.1, f32[3,1,65]{2,1,0:T(1,128)} %bitcast.9, s32[1,3]{1,0:T(1,128)} %dil_ref.1, ...), custom_call_target="tpu_custom_call" | custom-call | tf_op jit(solution)/shard_map/pallas_call | solution.py:395
  36.2 4.6 %shard_map.105 = (bf16[32,128,128]{2,1,0:T(8,128)(2,1)}, bf16[64,16,128]{2,1,0:T(8,128)(2,1)}) custom-call(bf16[32,160,128]{2,1,0:T(8,128)(2,1)} %bitcast.6, bf16[64,16,128]{2,1,0:T(8,128)(2,1)} %get-tuple-element.7.tr_ref, f32[25]{0:T(128)} %row_ref.3, f32[25]{0:T(128)} %col_ref.3), custom_call_target="tpu_custom_call" | custom-call | tf_op jit(solution)/shard_map/pallas_call | solution.py:445

commit v6 on v5

--- a/solution.py
+++ b/solution.py
@@ -438,7 +438,7 @@
         row_taps,
         col_taps,
     )
-    steps = frames // 4
+    steps = frames // 2
     few = padded[0] // steps
     share = traces.shape[0] // steps if traces.shape[0] % steps == 0 else 0
     part_spec = pl.BlockSpec((share,) + traces.shape[1:], lambda i: (i, 0, 0))

time: 41 us -> 43.4 us (1.059)
  Pallas kernels: 40.2 us -> 42.5 us
    pallas_call x1, Pallas kernels: 4.56 us -> 6.93 us  [on_device(): pl.pallas_call(functools.partial(adjoint_kernel, rim, edge), grid=(steps,...]
where the time goes in v6:
time: 43.4 us; the launch traced here: 43.2 us
  Pallas kernels  42.5 us (98%)
  between operations  0.64 us (1%)
    pallas_call x1, Pallas kernels, on_device(): pl.pallas_call(kernel, out_shape=(jax.ShapeDtypeStruct((planes_here, fram...  35.6 us
    pallas_call x1, Pallas kernels, on_device(): pl.pallas_call(functools.partial(adjoint_kernel, rim, edge), grid=(steps,...  6.93 us

profile of v6, /device:TPU:0, one launch (start us, length us, event | category | flops | bytes accessed | tf_op | source)
XLA Modules:
  0.0 43.2 jit_solution(13514432781162072190)
XLA Ops:
  0.6 35.6 %shard_map.104 = (bf16[2,16,160,128]{3,2,1,0:T(8,128)(2,1)}, bf16[64,16,128]{2,1,0:T(8,128)(2,1)}) custom-call(bf16[2,16,128,128]{3,2,1,0:T(8,128)(2,1)} %movie_ref.1, s32[8,16,128]{2,1,0:T(8,128)} %bitcast.7, s32[128]{0:T(128)} %bitcast.10, bf16[512,2,128]{2,1,0:T(2,128)(2,1)} %table_ref.1, f32[3,1,65]{2,1,0:T(1,128)} %bitcast.9, s32[1,3]{1,0:T(1,128)} %dil_ref.1, ...), custom_call_target="tpu_custom_call" | custom-call | tf_op jit(solution)/shard_map/pallas_call | solution.py:395
  36.2 6.9 %shard_map.105 = (bf16[32,128,128]{2,1,0:T(8,128)(2,1)}, bf16[64,16,128]{2,1,0:T(8,128)(2,1)}) custom-call(bf16[32,160,128]{2,1,0:T(8,128)(2,1)} %bitcast.6, bf16[64,16,128]{2,1,0:T(8,128)(2,1)} %get-tuple-element.7.tr_ref, f32[25]{0:T(128)} %row_ref.3, f32[25]{0:T(128)} %col_ref.3), custom_call_target="tpu_custom_call" | custom-call | tf_op jit(solution)/shard_map/pallas_call | solution.py:445
